TPU v7x, 512 devices: a whole 4x4x16 slice. The times are simulated.
512 devices in a mesh: cuts: 32 (over z, y_hi), angle: 16 (over y_lo, x, core).
Axes of the slice: x: 4, y: 4 (y_hi: 2, y_lo: 2; y = y_hi * 2 + y_lo), z: 16, core: 2. Of those that a mesh axis runs over, the one named last changes fastest.
Arguments:
- density: bfloat16 [32, 576, 256], P('cuts', 'angle'), may hold values from 0.049804688 to 2
- kernel_blocks: bfloat16 [576, 256, 384], P('cuts'), may hold values from -0.015625 to 0.015625
Outputs:
- sinogram: bfloat16 [32, 576, 384], P('cuts', 'angle')
All inputs are finite; a program needn't handle non-finite values.
Results may differ from a plain program's by a relative error of at most 0.0012.
Values may be sent and summed in bfloat16 or wider, within the bound.
No kernel may reach another device: no remote copies, remote signals or barrier semaphores. Data moves between devices by JAX's collectives and lax.ppermute only.
A program may use at most 64 MiB of HBM per device.

v0:
```python
import jax
import jax.numpy as jnp
from jax import lax
from jax.sharding import PartitionSpec as P


def local(density, kernel_blocks):
    angles_dev = density.shape[1]
    offsets_dev = kernel_blocks.shape[0]
    angle_count = lax.axis_size("angle")
    offset_start = lax.axis_index("cuts") * offsets_dev
    block_steps = offset_start // angles_dev
    remainder = offset_start - block_steps * angles_dev
    gathered = lax.all_gather(density, "cuts", axis=0, tiled=True)
    full_cycle = lax.all_gather(gathered, "angle", axis=1, tiled=True)
    doubled = jnp.concatenate([full_cycle, full_cycle[:, :angles_dev]], axis=1)
    window_start = (lax.axis_index("angle") - block_steps - 1) % angle_count * angles_dev
    window = lax.dynamic_slice_in_dim(doubled, window_start, 2 * angles_dev, 1)

    def shifted_rows(offset_lag):
        return lax.dynamic_slice_in_dim(window, angles_dev - remainder - offset_lag, angles_dev, 1)

    offset_lags = jnp.arange(offsets_dev, dtype=jnp.int32)
    stacked = jax.vmap(shifted_rows)(offset_lags)
    contribution = lax.psum_scatter(
        jnp.einsum("lsvr,lrb->svb", stacked, kernel_blocks, preferred_element_type=jnp.float32),
        "cuts",
        scatter_dimension=0,
        tiled=True,
    )
    return contribution.astype(jnp.bfloat16)


def solution(mesh):
    return jax.shard_map(
        local,
        mesh=mesh,
        in_specs=(P("cuts", "angle", None), P("cuts", None, None)),
        out_specs=P("cuts", "angle", None),
        check_vma=False,
    )
```

profile of v0, /device:TPU:6, one launch (start us, length us, event | category | flops | bytes accessed | tf_op | source)
XLA Modules:
  0.0 747.7 jit_solution(466443494181665318)
XLA Ops:
  6.5 0.0 copy-start
  6.5 0.0 all-gather.2.cloned.1.call-start
  6.5 86.7 %all_gather.6 = bf16[32,36,256]{2,1,0:T(8,128)(2,1)S(1)} all-gather(bf16[1,36,256]{2,1,0:T(8,128)(2,1)} %param.2), channel_id=1, replica_groups=mesh['cuts'=32,'angle'=16] {'cuts'}, dimensions={0}, use_global_device_ids=true | all-gather | bytes 608256 | tf_op jit(solution)/shard_map/all_gather | solution.py:14
  93.3 0.9 copy.5
  94.2 0.0 all-gather.2.cloned.1.call-update
  94.2 0.0 reduce-scatter.4.cloned.1.call-start
  94.3 57.7 %all-gather.2.cloned.1.call-done = bf16[32,576,256]{2,0,1:T(8,128)(2,1)} async-done(((bf16[32,36,256]{2,0,1:T(8,128)(2,1)}), bf16[32,576,256]{2,0,1:T(8,128)(2,1)}) %all-gather.2.cloned.1.call-update) | async-done | bytes 9437200 | tf_op jit(solution)/shard_map/all_gather | solution.py:15
  152.1 1.1 slice.7
  153.2 2.7 fusion.2
  155.9 7.0 gather_fusion
  162.9 0.0 copy-done
  162.9 8.4 %fusion = f32[32,36,384,1]{2,0,1,3:T(8,128)S(1)} fusion(bf16[18,32,36,256]{3,1,2,0:T(8,128)(2,1)} %gather_fusion, bf16[18,256,384]{2,1,0:T(8,128)(2,1)S(1)} %copy-done), kind=kOutput, calls=%fused_computation.3 | convolution fusion | flops 4076863488 | bytes 15925248 | tf_op jit(solution)/shard_map/lsvr,lrb->svb/dot_general | solution.py:26
  171.3 2.3 copy.11
  173.6 0.0 reduce-scatter.4.cloned.1.call-update
  173.6 565.8 %reduce-scatter.4.cloned.1.call-done = f32[1,36,384]{2,1,0:T(8,128)} async-done(((f32[32,36,384]{2,1,0:T(8,128)}), f32[1,36,384]{2,1,0:T(8,128)}) %reduce-scatter.4.cloned.1.call-update) | async-done | bytes 55312
  739.5 1.4 convert_element_type.3
  (1 shorter events, 0.0 us)
Async XLA Ops:
  6.5 156.4 %copy-start = (bf16[18,256,384]{2,1,0:T(8,128)(2,1)S(1)}, bf16[18,256,384]{2,1,0:T(8,128)(2,1)}, u32[]{:S(2)}) copy-start(bf16[18,256,384]{2,1,0:T(8,128)(2,1)} %param.3) | copy-start | bytes 10616836
  6.5 145.5 %all-gather.2.cloned.1.call-start = ((), (), s32[]{:S(2)}) async-start(), calls=%async_computation.1 | async-start | bytes 10027008 | tf_op jit(solution)/shard_map/all_gather | solution.py:15
  94.2 645.2 %reduce-scatter.4.cloned.1.call-start = ((), (), s32[]{:S(2)}) async-start(), calls=%async_computation.2 | async-start | bytes 2027520
Sparse Core Ops, SparseCore 0:
  94.3 57.6 all-gather.1
  173.7 565.6 reduce-scatter.3
where the time goes:
time: 748 us
  waiting for transfers between devices  624 us (83%)
  blocking collectives  86.7 us (12%)
  between operations  13.5 us (2%)
  local copies, waits for them, and re-layouts  11.4 us (2%)
  matrix products  8.36 us (1%)
    unnamed x3, waiting for transfers between devices  566 us
    all_gather x1, blocking collectives, local(): gathered = lax.all_gather(density, 'cuts', axis=0, tiled=True)  86.7 us
    all_gather x1, waiting for transfers between devices, local(): full_cycle = lax.all_gather(gathered, 'angle', axis=1, tiled=True)  57.7 us
  transfers between devices with their start and end apart: 2, of which 2 were waited for; matrix products, arithmetic and copies ran while one was open for 0% of the time, Pallas kernels for 0%

commit v1 on v0

v1 whole, which is shorter than its diff:
```python
import jax
import jax.numpy as jnp
from jax import lax
from jax.experimental import pallas as pl
from jax.experimental.pallas import tpu as pltpu
from jax.sharding import Mesh, PartitionSpec as P

CUTS = ("z", "yh")
ANGLE = ("yl", "x", "co")
NZ, NA, NR, NB = 16, 16, 16, 24
LANES = 128
F32, BF16 = jnp.float32, jnp.bfloat16


def rotate(tile, shift):
    shift %= LANES
    return tile if shift == 0 else pltpu.roll(tile, shift, 1)


def assemble(tiles, pieces, lane):
    cache = {}
    for get, src, dst, width in pieces:
        while width > 0:
            step = min(width, LANES - src % LANES, LANES - dst % LANES)
            shift = (dst - src) % LANES
            key = (id(get), src // LANES, shift)
            if key not in cache:
                cache[key] = rotate(get(src // LANES), shift)
            t, at = dst // LANES, dst % LANES
            if tiles[t] is None or step == LANES:
                tiles[t] = cache[key]
            else:
                tiles[t] = jnp.where((lane >= at) & (lane < at + step), cache[key], tiles[t])
            src, dst, width = src + step, dst + step, width - step
    return tiles


def pack_kernel(index_ref, k_ref, o_ref):
    del index_ref
    offsets = k_ref.shape[0]
    lane = lax.broadcasted_iota(jnp.int32, (NR, LANES), 1)
    cache = {}

    def reader(l):
        def get(t):
            if (l, t) not in cache:
                cache[l, t] = k_ref[l, :, t * LANES : (t + 1) * LANES].astype(F32)
            return cache[l, t]

        return get

    readers = [reader(l) for l in range(offsets)]
    width = offsets * NB
    for z in range(NZ):
        tiles = assemble(
            [None] * -(-width // LANES), [(readers[l], z * NB, l * NB, NB) for l in range(offsets)], lane
        )
        for t, tile in enumerate(tiles):
            w = min(LANES, width - t * LANES)
            o_ref[z, :, t * LANES : t * LANES + w] = tile[:, :w].astype(BF16)


def main_kernel(yh_ref, k1_ref, k2_ref, d_ref, o_ref, flat, weights, left, acc):
    half = k1_ref.shape[2]
    blocks = 2 * NZ * half // (NR * NB)
    tiles_all = 2 * NZ * half // LANES
    group = NR * NB // LANES
    lane = lax.broadcasted_iota(jnp.int32, (NR, LANES), 1)
    first = yh_ref[0] == 0

    def reader(z, h):
        cache = {}

        def get(t):
            if t not in cache:
                w = min(LANES, half - t * LANES)
                a = k1_ref[z, :, t * LANES : t * LANES + w].astype(F32)
                b = k2_ref[z, :, t * LANES : t * LANES + w].astype(F32)
                v = jnp.where(first, a, b) if h == 0 else jnp.where(first, b, a)
                if w < LANES:
                    v = jnp.concatenate([v, jnp.zeros((NR, LANES - w), F32)], axis=1)
                cache[t] = v
            return cache[t]

        return get

    tiles = assemble(
        [None] * tiles_all,
        [(reader(z, h), 0, (2 * z + h) * half, half) for z in range(NZ) for h in range(2)],
        lane,
    )
    for t in range(tiles_all):
        flat[t + group] = tiles[t]
    for t in range(group):
        flat[t] = tiles[tiles_all - group + t]

    for w in range(blocks):
        for t in range(2):
            for rep in range(2):
                left[(rep * blocks + w) * NZ : (rep * blocks + w + 1) * NZ, t * LANES : (t + 1) * LANES] = d_ref[2 * w + t]

    def build(block, carry):
        for j in range(NR):
            q, rem = divmod(NB * j, LANES)
            for t in range(group):
                at = block * group + t + group - q
                tile = flat[at]
                if rem:
                    tile = jnp.where(lane >= rem, rotate(tile, rem), rotate(flat[at - 1], rem))
                weights[block, j * NR : (j + 1) * NR, t * LANES : (t + 1) * LANES] = tile.astype(BF16)
        return carry

    lax.fori_loop(0, blocks, build, 0)
    acc[...] = jnp.zeros_like(acc)

    def step(block, carry):
        start = pl.multiple_of((blocks - block) * NZ, NZ)
        acc[...] += jnp.dot(left[pl.ds(start, blocks * NZ), :], weights[block], preferred_element_type=F32)
        return carry

    lax.fori_loop(0, blocks, step, 0)

    width = o_ref.shape[2]

    def out_tile(t):
        return acc[(t // group) * NZ : (t // group + 1) * NZ, (t % group) * LANES : (t % group + 1) * LANES]

    for a in range(NA):
        tiles = assemble([None] * -(-width // LANES), [(out_tile, a * width, 0, width)], lane)
        for t, tile in enumerate(tiles):
            w = min(LANES, width - t * LANES)
            o_ref[a, :, t * LANES : t * LANES + w] = tile[:, :w]


def pack(kernel_blocks, index):
    offsets, _, bins = kernel_blocks.shape
    return pl.pallas_call(
        pack_kernel,
        grid_spec=pltpu.PrefetchScalarGridSpec(
            num_scalar_prefetch=1,
            grid=(1,),
            in_specs=[pl.BlockSpec((offsets, NR, bins), lambda i, index: (0, index[0], 0))],
            out_specs=pl.BlockSpec((NZ, NR, offsets * NB), lambda i, index: (0, 0, 0)),
        ),
        out_shape=jax.ShapeDtypeStruct((NZ, NR, offsets * NB), BF16),
        compiler_params=pltpu.CompilerParams(vmem_limit_bytes=40 << 20),
        name="pack",
    )(index, kernel_blocks)


def project(yh, k1, k2, d):
    half = k1.shape[2]
    blocks = 2 * NZ * half // (NR * NB)
    width = 2 * NZ * half // NA
    vmem = pl.BlockSpec(memory_space=pltpu.VMEM)
    return pl.pallas_call(
        main_kernel,
        in_specs=[pl.BlockSpec(memory_space=pltpu.SMEM), vmem, vmem, vmem],
        out_specs=vmem,
        out_shape=jax.ShapeDtypeStruct((NA, NZ, width), F32),
        scratch_shapes=[
            pltpu.VMEM((2 * NZ * half // LANES + NR * NB // LANES, NR, LANES), F32),
            pltpu.VMEM((blocks, NR * NR, NR * NB), BF16),
            pltpu.VMEM((2 * blocks * NZ, NR * NR), BF16),
            pltpu.VMEM((blocks * NZ, NR * NB), F32),
        ],
        compiler_params=pltpu.CompilerParams(vmem_limit_bytes=40 << 20),
        name="project",
    )(yh, k1, k2, d)


def local(density, kernel_blocks):
    angles = density.shape[1]
    me = lax.axis_index(ANGLE).astype(jnp.int32).reshape(1)
    yh = lax.axis_index("yh").astype(jnp.int32).reshape(1)
    k1 = lax.all_to_all(pack(kernel_blocks, me), "z", 0, 0, tiled=True)
    k2 = lax.ppermute(k1, "yh", [(0, 1), (1, 0)])
    d = density.reshape(angles, NA, NR).transpose(1, 0, 2).reshape(NA, angles * NR)
    d = lax.all_to_all(d, ANGLE, 0, 0, tiled=True)
    d = d.reshape(1, -1, LANES)
    d = lax.all_to_all(jnp.broadcast_to(d, (NZ,) + d.shape[1:]), "z", 0, 0, tiled=True)
    d = d.transpose(1, 0, 2)
    parts = project(yh, k1, k2, d)
    parts = lax.all_to_all(parts, ANGLE, 0, 0, tiled=True)
    out = jnp.sum(parts, axis=0).astype(BF16)
    out = lax.all_to_all(out, "z", 0, 0, tiled=True)
    return out.reshape(NZ, angles, NB).transpose(1, 0, 2).reshape(1, angles, NZ * NB)


def solution(mesh):
    own = Mesh(mesh.devices.reshape(16, 2, 2, 4, 2), CUTS + ANGLE)
    return jax.shard_map(
        local,
        mesh=own,
        in_specs=(P(CUTS, ANGLE, None), P(CUTS, None, None)),
        out_specs=P(CUTS, ANGLE, None),
        check_vma=False,
    )
```

time: 748 us -> 131 us (0.18)
  the two profiles are of different devices: /device:TPU:6 before, /device:TPU:16 now
where the time goes in v1:
time: 131 us; the launch traced here: 130 us
  waiting for transfers between devices  38 us (29%)
  blocking collectives  36.1 us (28%)
  starting transfers between devices  28.8 us (22%)
  Pallas kernels  19 us (15%)
  local copies, waits for them, and re-layouts  6.58 us (5%)
  other arithmetic  1.55 us (1%)
    all_to_all x1, blocking collectives, local(): out = lax.all_to_all(out, 'z', 0, 0, tiled=True)  18.6 us
    all_to_all x1, waiting for transfers between devices, local(): k1 = lax.all_to_all(pack(kernel_blocks, me), 'z', 0, 0, tiled=True)  18.2 us
    pallas_call x1, Pallas kernels, project(): pl.pallas_call(main_kernel, in_specs=[pl.BlockSpec(memory_space=pltpu.SME...  17.9 us
    all_to_all x1, blocking collectives, local(): parts = lax.all_to_all(parts, ANGLE, 0, 0, tiled=True)  17.5 us
    all_to_all x1, waiting for transfers between devices, local(): lax.all_to_all(jnp.broadcast_to(d, (NZ,) + d.shape[1:]), 'z', 0, 0, tiled...  16.8 us
    all_to_all x1, starting transfers between devices, local(): k1 = lax.all_to_all(pack(kernel_blocks, me), 'z', 0, 0, tiled=True)  15.2 us
    all_to_all x1, starting transfers between devices, local(): lax.all_to_all(jnp.broadcast_to(d, (NZ,) + d.shape[1:]), 'z', 0, 0, tiled...  5.94 us
    all_to_all x1, starting transfers between devices, local(): d = lax.all_to_all(d, ANGLE, 0, 0, tiled=True)  5.12 us
  transfers between devices with their start and end apart: 4, of which 3 were waited for; matrix products, arithmetic and copies ran while one was open for 0% of the time, Pallas kernels for 1%

profile of v1, /device:TPU:16, one launch (start us, length us, event | category | flops | bytes accessed | tf_op | source)
XLA Modules:
  0.0 130.1 jit_solution(1191086010998275639)
XLA Ops:
  0.0 0.9 copy.11
  0.9 0.2 copy.12
  1.1 0.2 all_to_all.25
  1.2 0.5 broadcast.2
  1.7 0.7 reduce.2
  2.4 0.7 reshape.40
  3.1 5.1 %all-to-all-start.1 = ((bf16[16,2,288]{2,1,0:T(2,128)(2,1)}), bf16[16,2,288]{2,1,0:T(2,128)(2,1)S(1)}, u32[]{:S(2)}, u32[]{:S(2)}) async-start(bf16[16,2,288]{2,1,0:T(2,128)(2,1)} %reshape.40), calls=%async_computation.1 | async-start | bytes 49152 | tf_op jit(solution)/shard_map/all_to_all | solution.py:179
  8.2 2.0 %copy-done = bf16[18,256,384]{2,1,0:T(8,128)(2,1)S(1)} copy-done((bf16[18,256,384]{2,1,0:T(8,128)(2,1)S(1)}, bf16[18,256,384]{2,1,0:T(8,128)(2,1)}, u32[]{:S(2)}) %copy-start) | copy-done | bytes 3538968
  10.2 1.1 pack.1
  11.3 3.0 %all-to-all-done.1 = bf16[16,2,288]{2,1,0:T(2,128)(2,1)S(1)} async-done(((bf16[16,2,288]{2,1,0:T(2,128)(2,1)}), bf16[16,2,288]{2,1,0:T(2,128)(2,1)S(1)}, u32[]{:S(2)}, u32[]{:S(2)}) %all-to-all-start.1) | async-done | bytes 18464 | tf_op jit(solution)/shard_map/all_to_all | solution.py:179
  14.3 15.2 %all-to-all-start = ((bf16[16,16,432]{2,1,0:T(8,128)(2,1)}), bf16[16,16,432]{2,1,0:T(8,128)(2,1)S(1)}, u32[]{:S(2)}, u32[]{:S(2)}) async-start(bf16[16,16,432]{2,1,0:T(8,128)(2,1)} %pack.1), calls=%async_computation | async-start | bytes 524288 | tf_op jit(solution)/shard_map/all_to_all | solution.py:176
  29.6 0.1 reduce
  29.8 18.2 %all-to-all-done.k1_ref = bf16[16,16,432]{2,1,0:T(8,128)(2,1)S(1)} async-done(((bf16[16,16,432]{2,1,0:T(8,128)(2,1)}), bf16[16,16,432]{2,1,0:T(8,128)(2,1)S(1)}, u32[]{:S(2)}, u32[]{:S(2)}) %all-to-all-start) | async-done | bytes 221216 | tf_op jit(solution)/shard_map/all_to_all | solution.py:176
  48.0 0.7 broadcast_in_dim.8
  48.7 5.9 %all-to-all-start.2 = ((bf16[16,72,128]{2,1,0:T(8,128)(2,1)}), bf16[16,72,128]{2,1,0:T(8,128)(2,1)S(1)}, u32[]{:S(2)}, u32[]{:S(2)}) async-start(bf16[16,72,128]{2,1,0:T(8,128)(2,1)} %broadcast_in_dim.8), calls=%async_computation.2 | async-start | bytes 589824 | tf_op jit(solution)/shard_map/all_to_all | solution.py:181
  54.7 2.5 %collective-permute-start = (bf16[16,16,432]{2,1,0:T(8,128)(2,1)S(1)}, bf16[16,16,432]{2,1,0:T(8,128)(2,1)S(1)}, u32[]{:S(2)}, u32[]{:S(2)}) collective-permute-start(bf16[16,16,432]{2,1,0:T(8,128)(2,1)S(1)} %all-to-all-done.k1_ref), channel_id=1, source_target_pairs={{0,16},{16,0},{1,17},{17,1},{2,18},{18,2},{3,19},{19,3},{4,20},{20... | collective-permute-start | bytes 663560 | tf_op jit(solution)/shard_map/ppermute | solution.py:177
  57.2 16.8 %all-to-all-done.2 = bf16[16,72,128]{2,1,0:T(8,128)(2,1)S(1)} async-done(((bf16[16,72,128]{2,1,0:T(8,128)(2,1)}), bf16[16,72,128]{2,1,0:T(8,128)(2,1)S(1)}, u32[]{:S(2)}, u32[]{:S(2)}) %all-to-all-start.2) | async-done | bytes 294944 | tf_op jit(solution)/shard_map/all_to_all | solution.py:181
  74.1 17.9 %project.1 = f32[16,16,864]{2,1,0:T(8,128)S(1)} custom-call(s32[1]{0:T(128)} %bitcast.yh_ref, bf16[16,16,432]{2,1,0:T(8,128)(2,1)S(1)} %all-to-all-done.k1_ref, bf16[16,16,432]{2,1,0:T(8,128)(2,1)S(1)} %collective-permute-done.k2_ref, bf16[72,16,128]{2,1,0:T(8,128)(2,1)S(1)} %bitcast.12), custom_call_target="tpu_custom_call" | custom-call | tf_op jit(solution)/shard_map/project/pallas_call | solution.py:156
  92.0 17.5 %all_to_all.31 = f32[16,16,864]{2,1,0:T(8,128)S(1)} all-to-all(f32[16,16,864]{2,1,0:T(8,128)S(1)} %project.1), channel_id=1, replica_groups=mesh['z'=16,'yh'=2,'yl'=2,'x'=4,'co'=2] {'yl','x','co'}, dimensions={0} | all-to-all | bytes 1769472 | tf_op jit(solution)/shard_map/all_to_all | solution.py:184
  109.6 0.6 reduce.3
  110.2 18.6 %all_to_all.32 = bf16[16,2,432]{2,1,0:T(2,128)(2,1)S(1)} all-to-all(bf16[16,2,432]{2,1,0:T(2,128)(2,1)S(1)} %reshape.42), channel_id=1, replica_groups=mesh['z'=16,'yh'=2,'yl'=2,'x'=4,'co'=2] {'z'}, dimensions={0} | all-to-all | bytes 55296 | tf_op jit(solution)/shard_map/all_to_all | solution.py:186
  129.0 0.2 reduce.1
  129.1 0.2 reshape.36
  129.4 0.8 reshape.37
  (9 shorter events, 0.5 us)
Async XLA Ops:
  3.1 11.2 %all-to-all-start.1 = ((bf16[16,2,288]{2,1,0:T(2,128)(2,1)}), bf16[16,2,288]{2,1,0:T(2,128)(2,1)S(1)}, u32[]{:S(2)}, u32[]{:S(2)}) async-start(bf16[16,2,288]{2,1,0:T(2,128)(2,1)} %reshape.40), calls=%async_computation.1 | async-start | bytes 49152 | tf_op jit(solution)/shard_map/all_to_all | solution.py:179
  8.2 2.0 %copy-start = (bf16[18,256,384]{2,1,0:T(8,128)(2,1)S(1)}, bf16[18,256,384]{2,1,0:T(8,128)(2,1)}, u32[]{:S(2)}) copy-start(bf16[18,256,384]{2,1,0:T(8,128)(2,1)} %k_ref.1) | copy-start | bytes 10616836
  14.3 33.7 %all-to-all-start = ((bf16[16,16,432]{2,1,0:T(8,128)(2,1)}), bf16[16,16,432]{2,1,0:T(8,128)(2,1)S(1)}, u32[]{:S(2)}, u32[]{:S(2)}) async-start(bf16[16,16,432]{2,1,0:T(8,128)(2,1)} %pack.1), calls=%async_computation | async-start | bytes 524288 | tf_op jit(solution)/shard_map/all_to_all | solution.py:176
  48.7 25.3 %all-to-all-start.2 = ((bf16[16,72,128]{2,1,0:T(8,128)(2,1)}), bf16[16,72,128]{2,1,0:T(8,128)(2,1)S(1)}, u32[]{:S(2)}, u32[]{:S(2)}) async-start(bf16[16,72,128]{2,1,0:T(8,128)(2,1)} %broadcast_in_dim.8), calls=%async_computation.2 | async-start | bytes 589824 | tf_op jit(solution)/shard_map/all_to_all | solution.py:181
  54.7 19.4 %collective-permute-start = (bf16[16,16,432]{2,1,0:T(8,128)(2,1)S(1)}, bf16[16,16,432]{2,1,0:T(8,128)(2,1)S(1)}, u32[]{:S(2)}, u32[]{:S(2)}) collective-permute-start(bf16[16,16,432]{2,1,0:T(8,128)(2,1)S(1)} %all-to-all-done.k1_ref), channel_id=1, source_target_pairs={{0,16},{16,0},{1,17},{17,1},{2,18},{18,2},{3,19},{19,3},{4,20},{20... | collective-permute-start | bytes 663560 | tf_op jit(solution)/shard_map/ppermute | solution.py:177

commit v2 on v1

v2 whole, which is shorter than its diff:
```python
import jax
import jax.numpy as jnp
from jax import lax
from jax.experimental import pallas as pl
from jax.experimental.pallas import tpu as pltpu
from jax.sharding import Mesh, PartitionSpec as P

CUTS = ("z", "yh")
ANGLE = ("yl", "x", "co")
NZ, NA, NR, NB = 16, 16, 16, 24
ROWS, LANES = 16, 128
F32, BF16 = jnp.float32, jnp.bfloat16
VMEM_BYTES = 40 << 20


def rotate(tile, shift):
    shift %= LANES
    return tile if shift == 0 else pltpu.roll(tile, shift, 1)


def assemble(count, pieces):
    lane = lax.broadcasted_iota(jnp.int32, (ROWS, LANES), 1)
    tiles, cache = [None] * count, {}
    for n, (get, src, dst, width) in enumerate(pieces):
        while width > 0:
            step = min(width, LANES - src % LANES, LANES - dst % LANES)
            key = (id(get), src // LANES, (dst - src) % LANES)
            if key not in cache:
                cache[key] = rotate(get(src // LANES), dst - src)
            t, at = dst // LANES, dst % LANES
            if tiles[t] is None or step == LANES:
                tiles[t] = cache[key]
            else:
                tiles[t] = jnp.where((lane >= at) & (lane < at + step), cache[key], tiles[t])
            src, dst, width = src + step, dst + step, width - step
    return tiles


def cached(load):
    seen = {}

    def get(t):
        if t not in seen:
            seen[t] = load(t)
        return seen[t]

    return get


def density_tiles(angles):
    spots, group = [], 0
    for first in range(0, angles, ROWS):
        count = min(ROWS, angles - first)
        if count == ROWS:
            spots += [(first, count, 0, group, 0), (first, count, 1, group + 1, 0)]
            group += 2
        else:
            assert 2 * count <= ROWS
            spots += [(first, count, 0, group, 0), (first, count, 1, group, count)]
            group += 1
    return spots, group


def pack_kernel(index_ref, k_ref, d_ref, o_ref):
    del index_ref
    offsets, angles = k_ref.shape[0], d_ref.shape[0]
    width = offsets * NB
    groups = -(-width // LANES)
    readers = [
        cached(lambda t, l=l: k_ref[l, :, t * LANES : (t + 1) * LANES].astype(F32)) for l in range(offsets)
    ]
    for z in range(NZ):
        tiles = assemble(groups, [(readers[l], z * NB, l * NB, NB) for l in range(offsets)])
        for t, tile in enumerate(tiles):
            o_ref[z, t] = tile.astype(BF16)
    rows = {}
    for first, count, half, group, row in density_tiles(angles)[0]:
        rows.setdefault(group, []).append(
            d_ref[first : first + count, half * LANES : (half + 1) * LANES].astype(F32)
        )
    for group, parts in rows.items():
        have = sum(p.shape[0] for p in parts)
        if have < ROWS:
            parts = parts + [jnp.zeros((ROWS - have, LANES), F32)]
        tile = (parts[0] if len(parts) == 1 else jnp.concatenate(parts, axis=0)).astype(BF16)
        for z in range(NZ):
            o_ref[z, groups + group] = tile


def regroup_kernel(d_ref, o_ref):
    angles = o_ref.shape[1] * LANES // NR
    spots, _ = density_tiles(36)
    per = LANES // NR
    lane = lax.broadcasted_iota(jnp.int32, (NZ, LANES), 1)
    masks = [(lane >= p * NR) & (lane < (p + 1) * NR) for p in range(per)]
    out = {}
    for first, count, half, group, row in spots:
        for i in range(count):
            t, p = divmod(first + i, per)
            tile = d_ref[group, row + i]
            for k in range(per):
                turned = rotate(tile, (p - k) * NR)
                key = (half * per + k, t)
                out[key] = turned if key not in out else jnp.where(masks[p], turned, out[key])
    del angles
    for (a, t), tile in out.items():
        o_ref[a, t] = tile


def main_kernel(yh_ref, k1_ref, k2_ref, d_ref, o_ref, flat, weights, left):
    half = 18 * NB
    group = NR * NB // LANES
    tiles_all = 2 * NZ * half // LANES
    blocks = tiles_all // group
    width = o_ref.shape[2]
    lane = lax.broadcasted_iota(jnp.int32, (ROWS, LANES), 1)
    first = yh_ref[0] == 0

    def reader(z, h):
        def load(t):
            a, b = k1_ref[z, t].astype(F32), k2_ref[z, t].astype(F32)
            return jnp.where(first, a, b) if h == 0 else jnp.where(first, b, a)

        return cached(load)

    tiles = assemble(
        tiles_all, [(reader(z, h), 0, (2 * z + h) * half, half) for z in range(NZ) for h in range(2)]
    )
    for t in range(tiles_all):
        flat[t + group] = tiles[t]
    for t in range(group):
        flat[t] = tiles[tiles_all - group + t]

    span = width * NR // NB
    tiles = assemble(
        blocks * 2, [(cached(lambda t, a=a: d_ref[a, t].astype(F32)), 0, a * span, span) for a in range(NA)]
    )
    for w in range(blocks):
        for t in range(2):
            tile = tiles[2 * w + t].astype(BF16)
            for rep in range(2):
                row = (rep * blocks + w) * NZ
                left[row : row + NZ, t * LANES : (t + 1) * LANES] = tile

    for block in range(blocks):
        for j in range(NR):
            q, rem = divmod(NB * j, LANES)
            base = block * group + group - q
            if rem:
                turned = [rotate(flat[base + t - 1], rem) for t in range(group + 1)]
                outs = [jnp.where(lane >= rem, turned[t + 1], turned[t]) for t in range(group)]
            else:
                outs = [flat[base + t] for t in range(group)]
            for t in range(group):
                weights[block, j * NR : (j + 1) * NR, t * LANES : (t + 1) * LANES] = outs[t].astype(BF16)
    lhs = [left[(blocks - c) * NZ : (2 * blocks - c) * NZ, :] for c in range(blocks)]
    acc = jnp.dot(
        jnp.concatenate(lhs, axis=1),
        weights[...].reshape(blocks * NR * NR, NR * NB),
        preferred_element_type=F32,
    )

    def out_tile(t):
        return acc[(t // group) * NZ : (t // group + 1) * NZ, (t % group) * LANES : (t % group + 1) * LANES]

    for a in range(NA):
        tiles = assemble(-(-width // LANES), [(out_tile, a * width, 0, width)])
        for t, tile in enumerate(tiles):
            w = min(LANES, width - t * LANES)
            o_ref[a, :, t * LANES : t * LANES + w] = tile[:, :w]


def pack(kernel_blocks, density, index):
    offsets, _, bins = kernel_blocks.shape
    angles, radii = density.shape
    groups = -(-offsets * NB // LANES) + density_tiles(angles)[1]
    return pl.pallas_call(
        pack_kernel,
        grid_spec=pltpu.PrefetchScalarGridSpec(
            num_scalar_prefetch=1,
            grid=(1,),
            in_specs=[
                pl.BlockSpec((offsets, NR, bins), lambda i, index: (0, index[0], 0)),
                pl.BlockSpec((angles, radii), lambda i, index: (0, 0)),
            ],
            out_specs=pl.BlockSpec((NZ, groups, ROWS, LANES), lambda i, index: (0, 0, 0, 0)),
        ),
        out_shape=jax.ShapeDtypeStruct((NZ, groups, ROWS, LANES), BF16),
        compiler_params=pltpu.CompilerParams(vmem_limit_bytes=VMEM_BYTES),
        name="pack",
    )(index, kernel_blocks, density)


def regroup(d):
    vmem = pl.BlockSpec(memory_space=pltpu.VMEM)
    return pl.pallas_call(
        regroup_kernel,
        in_specs=[vmem],
        out_specs=vmem,
        out_shape=jax.ShapeDtypeStruct((NA, d.shape[0], NZ, LANES), BF16),
        compiler_params=pltpu.CompilerParams(vmem_limit_bytes=VMEM_BYTES),
        name="regroup",
    )(d)


def project(yh, k1, k2, d):
    half = 18 * NB
    blocks = 2 * NZ * half // (NR * NB)
    width = 2 * NZ * half // NA
    vmem = pl.BlockSpec(memory_space=pltpu.VMEM)
    return pl.pallas_call(
        main_kernel,
        in_specs=[pl.BlockSpec(memory_space=pltpu.SMEM), vmem, vmem, vmem],
        out_specs=vmem,
        out_shape=jax.ShapeDtypeStruct((NA, NZ, width), F32),
        scratch_shapes=[
            pltpu.VMEM((2 * NZ * half // LANES + NR * NB // LANES, ROWS, LANES), F32),
            pltpu.VMEM((blocks, NR * NR, NR * NB), BF16),
            pltpu.VMEM((2 * blocks * NZ, NR * NR), BF16),
        ],
        compiler_params=pltpu.CompilerParams(vmem_limit_bytes=VMEM_BYTES),
        name="project",
    )(yh, k1, k2, d)


def local(density, kernel_blocks):
    offsets, angles = kernel_blocks.shape[0], density.shape[1]
    me = lax.axis_index(ANGLE).astype(jnp.int32).reshape(1)
    yh = lax.axis_index("yh").astype(jnp.int32).reshape(1)
    both = lax.all_to_all(pack(kernel_blocks, density[0], me), "z", 0, 0, tiled=True)
    groups = -(-offsets * NB // LANES)
    k1 = both[:, :groups]
    k2 = lax.ppermute(k1, "yh", [(0, 1), (1, 0)])
    d = regroup(both[:, groups:].transpose(1, 2, 0, 3))
    d = lax.all_to_all(d, ANGLE, 0, 0, tiled=True)
    parts = project(yh, k1, k2, d)
    parts = lax.all_to_all(parts, ANGLE, 0, 0, tiled=True)
    out = jnp.sum(parts, axis=0).astype(BF16)
    out = lax.all_to_all(out, "z", 0, 0, tiled=True)
    return out.reshape(NZ, angles, NB).transpose(1, 0, 2).reshape(1, angles, NZ * NB)


def solution(mesh):
    own = Mesh(mesh.devices.reshape(16, 2, 2, 4, 2), CUTS + ANGLE)
    return jax.shard_map(
        local,
        mesh=own,
        in_specs=(P(CUTS, ANGLE, None), P(CUTS, None, None)),
        out_specs=P(CUTS, ANGLE, None),
        check_vma=False,
    )
```

time: 131 us -> 117 us (0.89)
  the two profiles are of different devices: /device:TPU:16 before, /device:TPU:1 now
where the time goes in v2:
time: 117 us
  blocking collectives  80.3 us (69%)
  starting transfers between devices  13.5 us (12%)
  waiting for transfers between devices  9.28 us (8%)
  Pallas kernels  7.92 us (7%)
  local copies, waits for them, and re-layouts  4.57 us (4%)
    all_to_all x1, blocking collectives, local(): lax.all_to_all(pack(kernel_blocks, density[0], me), 'z', 0, 0, tiled=True)  47.8 us
    all_to_all x1, blocking collectives, local(): parts = lax.all_to_all(parts, ANGLE, 0, 0, tiled=True)  18.2 us
    all_to_all x1, blocking collectives, local(): out = lax.all_to_all(out, 'z', 0, 0, tiled=True)  14.3 us
    ppermute x1, waiting for transfers between devices, local(): k2 = lax.ppermute(k1, 'yh', [(0, 1), (1, 0)])  9.28 us
    all_to_all x1, starting transfers between devices, local(): d = lax.all_to_all(d, ANGLE, 0, 0, tiled=True)  8.94 us
    pallas_call x1, Pallas kernels, project(): pl.pallas_call(main_kernel, in_specs=[pl.BlockSpec(memory_space=pltpu.SME...  6.18 us
    ppermute x1, starting transfers between devices, local(): k2 = lax.ppermute(k1, 'yh', [(0, 1), (1, 0)])  4.55 us
    unnamed x6, local copies, waits for them, and re-layouts  2.95 us
  transfers between devices with their start and end apart: 2, of which 1 were waited for; matrix products, arithmetic and copies ran while one was open for 0% of the time, Pallas kernels for 0%

profile of v2, /device:TPU:1, one launch (start us, length us, event | category | flops | bytes accessed | tf_op | source)
XLA Modules:
  0.0 116.5 jit_solution(10001779866302100918)
XLA Ops:
  0.0 0.0 copy-start
  0.0 2.0 %copy-done = bf16[18,256,384]{2,1,0:T(8,128)(2,1)S(1)} copy-done((bf16[18,256,384]{2,1,0:T(8,128)(2,1)S(1)}, bf16[18,256,384]{2,1,0:T(8,128)(2,1)}, u32[]{:S(2)}) %copy-start) | copy-done | bytes 3538968
  2.0 0.0 copy-start.1
  2.0 0.7 copy-done.1
  2.7 0.4 pack.1
  3.2 47.8 %all_to_all.21 = bf16[16,9,16,128]{3,2,1,0:T(8,128)(2,1)S(1)} all-to-all(bf16[16,9,16,128]{3,2,1,0:T(8,128)(2,1)S(1)} %pack.1), channel_id=1, replica_groups=mesh['z'=16,'yh'=2,'yl'=2,'x'=4,'co'=2] {'z'}, dimensions={0} | all-to-all | bytes 1179648 | tf_op jit(solution)/shard_map/all_to_all | solution.py:230
  51.0 0.1 copy.8.d_ref
  51.1 1.3 %regroup.1 = bf16[16,5,16,128]{3,2,1,0:T(8,128)(2,1)} custom-call(bf16[5,16,16,128]{3,2,1,0:T(8,128)(2,1)S(1)} %copy.8.d_ref), custom_call_target="tpu_custom_call" | custom-call | tf_op jit(solution)/shard_map/regroup/pallas_call | solution.py:196
  52.4 8.9 %all-to-all-start.1 = ((bf16[16,5,16,128]{3,2,1,0:T(8,128)(2,1)}), bf16[16,5,16,128]{3,2,1,0:T(8,128)(2,1)S(1)}, u32[]{:S(2)}, u32[]{:S(2)}) async-start(bf16[16,5,16,128]{3,2,1,0:T(8,128)(2,1)} %regroup.1), calls=%async_computation.1 | async-start | bytes 655360 | tf_op jit(solution)/shard_map/all_to_all | solution.py:235
  61.4 4.5 %collective-permute-start = (bf16[16,4,16,128]{3,2,1,0:T(8,128)(2,1)S(1)}, bf16[16,4,16,128]{3,2,1,0:T(8,128)(2,1)S(1)}, u32[]{:S(2)}, u32[]{:S(2)}) collective-permute-start(bf16[16,4,16,128]{3,2,1,0:T(8,128)(2,1)S(1)} %slice.8.k1_ref), channel_id=1, source_target_pairs={{0,16},{16,0},{1,17},{17,1},{2,18},{18,2},{3,19},{19,3},{4,20},{20... | collective-permute-start | bytes 786440 | tf_op jit(solution)/shard_map/ppermute | solution.py:233
  65.9 9.3 %collective-permute-done.k2_ref = bf16[16,4,16,128]{3,2,1,0:T(8,128)(2,1)S(1)} collective-permute-done((bf16[16,4,16,128]{3,2,1,0:T(8,128)(2,1)S(1)}, bf16[16,4,16,128]{3,2,1,0:T(8,128)(2,1)S(1)}, u32[]{:S(2)}, u32[]{:S(2)}) %collective-permute-start) | collective-permute-done | bytes 262176 | tf_op jit(solution)/shard_map/ppermute | solution.py:233
  75.2 0.0 all-to-all-done.1.d_ref
  75.2 6.2 %project.1 = f32[16,16,864]{2,1,0:T(8,128)S(1)} custom-call(s32[1]{0:T(128)} %bitcast.yh_ref, bf16[16,4,16,128]{3,2,1,0:T(8,128)(2,1)S(1)} %slice.8.k1_ref, bf16[16,4,16,128]{3,2,1,0:T(8,128)(2,1)S(1)} %collective-permute-done.k2_ref, bf16[16,5,16,128]{3,2,1,0:T(8,128)(2,1)S(1)} %all-to-all-done.1.d_ref), custom_call_target="tpu_custom_call" | custom-call | tf_op jit(solution)/shard_map/project/pallas_call | solution.py:211
  81.4 18.2 %all_to_all.22 = f32[16,16,864]{2,1,0:T(8,128)S(1)} all-to-all(f32[16,16,864]{2,1,0:T(8,128)S(1)} %project.1), channel_id=1, replica_groups=mesh['z'=16,'yh'=2,'yl'=2,'x'=4,'co'=2] {'yl','x','co'}, dimensions={0} | all-to-all | bytes 1769472 | tf_op jit(solution)/shard_map/all_to_all | solution.py:237
  99.6 0.1 reduce_sum.9
  99.6 0.5 broadcast.1
  100.2 0.7 reduce.1
  100.8 0.1 reshape.28
  100.9 14.3 %all_to_all.23 = bf16[16,2,432]{2,1,0:T(2,128)(2,1)S(1)} all-to-all(bf16[16,2,432]{2,1,0:T(2,128)(2,1)S(1)} %reshape.28), channel_id=1, replica_groups=mesh['z'=16,'yh'=2,'yl'=2,'x'=4,'co'=2] {'z'}, dimensions={0} | all-to-all | bytes 55296 | tf_op jit(solution)/shard_map/all_to_all | solution.py:239
  115.2 0.1 reshape.29
  115.3 0.2 reduce
  115.5 0.2 reshape.25
  115.7 0.8 reshape.26
  (3 shorter events, 0.1 us)
Async XLA Ops:
  0.0 2.0 %copy-start = (bf16[18,256,384]{2,1,0:T(8,128)(2,1)S(1)}, bf16[18,256,384]{2,1,0:T(8,128)(2,1)}, u32[]{:S(2)}) copy-start(bf16[18,256,384]{2,1,0:T(8,128)(2,1)} %k_ref.1) | copy-start | bytes 10616836
  2.0 0.7 copy-start.1
  52.4 22.8 %all-to-all-start.1 = ((bf16[16,5,16,128]{3,2,1,0:T(8,128)(2,1)}), bf16[16,5,16,128]{3,2,1,0:T(8,128)(2,1)S(1)}, u32[]{:S(2)}, u32[]{:S(2)}) async-start(bf16[16,5,16,128]{3,2,1,0:T(8,128)(2,1)} %regroup.1), calls=%async_computation.1 | async-start | bytes 655360 | tf_op jit(solution)/shard_map/all_to_all | solution.py:235
  61.4 13.8 %collective-permute-start = (bf16[16,4,16,128]{3,2,1,0:T(8,128)(2,1)S(1)}, bf16[16,4,16,128]{3,2,1,0:T(8,128)(2,1)S(1)}, u32[]{:S(2)}, u32[]{:S(2)}) collective-permute-start(bf16[16,4,16,128]{3,2,1,0:T(8,128)(2,1)S(1)} %slice.8.k1_ref), channel_id=1, source_target_pairs={{0,16},{16,0},{1,17},{17,1},{2,18},{18,2},{3,19},{19,3},{4,20},{20... | collective-permute-start | bytes 786440 | tf_op jit(solution)/shard_map/ppermute | solution.py:233

commit v3 on v2

--- a/solution.py
+++ b/solution.py
@@ -8,7 +8,9 @@
 CUTS = ("z", "yh")
 ANGLE = ("yl", "x", "co")
 NZ, NA, NR, NB = 16, 16, 16, 24
+OFFSETS, VIEWS = 18, 36
 ROWS, LANES = 16, 128
+TAIL = OFFSETS * NB % LANES
 F32, BF16 = jnp.float32, jnp.bfloat16
 VMEM_BYTES = 40 << 20
 
@@ -47,68 +49,57 @@
     return get
 
 
-def density_tiles(angles):
-    spots, group = [], 0
-    for first in range(0, angles, ROWS):
-        count = min(ROWS, angles - first)
-        if count == ROWS:
-            spots += [(first, count, 0, group, 0), (first, count, 1, group + 1, 0)]
-            group += 2
-        else:
-            assert 2 * count <= ROWS
-            spots += [(first, count, 0, group, 0), (first, count, 1, group, count)]
-            group += 1
-    return spots, group
-
-
-def pack_kernel(index_ref, k_ref, d_ref, o_ref):
-    del index_ref
-    offsets, angles = k_ref.shape[0], d_ref.shape[0]
-    width = offsets * NB
-    groups = -(-width // LANES)
+def pack_kernel(mine_ref, yh_ref, k_hbm, d_hbm, o_ref, k_ref, d_ref, sems):
+    radii = pl.ds(pl.multiple_of(mine_ref[0] * NR, NR), NR)
+    copies = [
+        pltpu.make_async_copy(k_hbm.at[:, radii, :], k_ref, sems.at[0]),
+        pltpu.make_async_copy(d_hbm.at[0], d_ref, sems.at[1]),
+    ]
+    for copy in copies:
+        copy.start()
+    swap = yh_ref[0] == 1
+    copies[1].wait()
+    low, high = d_ref[:, :LANES].astype(F32), d_ref[:, LANES:].astype(F32)
+    halves = jnp.where(swap, high, low), jnp.where(swap, low, high)
+    for n in range(2):
+        for h in range(2):
+            tile = halves[h][n * ROWS : (n + 1) * ROWS].astype(BF16)
+            for z in range(NZ):
+                o_ref[z, 4 + 2 * n + h] = tile
+    rest = [h[2 * ROWS :] for h in halves]
+    copies[0].wait()
     readers = [
-        cached(lambda t, l=l: k_ref[l, :, t * LANES : (t + 1) * LANES].astype(F32)) for l in range(offsets)
+        cached(lambda t, l=l: k_ref[l, :, t * LANES : (t + 1) * LANES].astype(F32)) for l in range(OFFSETS)
     ]
+    lane = lax.broadcasted_iota(jnp.int32, (ROWS // 2, LANES), 1)
     for z in range(NZ):
-        tiles = assemble(groups, [(readers[l], z * NB, l * NB, NB) for l in range(offsets)])
-        for t, tile in enumerate(tiles):
-            o_ref[z, t] = tile.astype(BF16)
-    rows = {}
-    for first, count, half, group, row in density_tiles(angles)[0]:
-        rows.setdefault(group, []).append(
-            d_ref[first : first + count, half * LANES : (half + 1) * LANES].astype(F32)
-        )
-    for group, parts in rows.items():
-        have = sum(p.shape[0] for p in parts)
-        if have < ROWS:
-            parts = parts + [jnp.zeros((ROWS - have, LANES), F32)]
-        tile = (parts[0] if len(parts) == 1 else jnp.concatenate(parts, axis=0)).astype(BF16)
-        for z in range(NZ):
-            o_ref[z, groups + group] = tile
+        tiles = assemble(4, [(readers[l], z * NB, l * NB, NB) for l in range(OFFSETS)])
+        for t in range(3):
+            o_ref[z, t] = tiles[t].astype(BF16)
+        last = jnp.where(lane < TAIL, tiles[3][: ROWS // 2], rotate(tiles[3][ROWS // 2 :], TAIL))
+        o_ref[z, 3] = jnp.concatenate([last] + rest, axis=0).astype(BF16)
 
 
 def regroup_kernel(d_ref, o_ref):
-    angles = o_ref.shape[1] * LANES // NR
-    spots, _ = density_tiles(36)
     per = LANES // NR
     lane = lax.broadcasted_iota(jnp.int32, (NZ, LANES), 1)
     masks = [(lane >= p * NR) & (lane < (p + 1) * NR) for p in range(per)]
     out = {}
-    for first, count, half, group, row in spots:
-        for i in range(count):
-            t, p = divmod(first + i, per)
-            tile = d_ref[group, row + i]
+    for angle in range(VIEWS):
+        n, i = divmod(angle, ROWS)
+        t, p = divmod(angle, per)
+        for h in range(2):
+            tile = d_ref[1 + 2 * n + h, i] if n < 2 else d_ref[0, ROWS // 2 + (VIEWS - 2 * ROWS) * h + i]
             for k in range(per):
                 turned = rotate(tile, (p - k) * NR)
-                key = (half * per + k, t)
+                key = (h * per + k, t)
                 out[key] = turned if key not in out else jnp.where(masks[p], turned, out[key])
-    del angles
     for (a, t), tile in out.items():
         o_ref[a, t] = tile
 
 
 def main_kernel(yh_ref, k1_ref, k2_ref, d_ref, o_ref, flat, weights, left):
-    half = 18 * NB
+    half = OFFSETS * NB
     group = NR * NB // LANES
     tiles_all = 2 * NZ * half // LANES
     blocks = tiles_all // group
@@ -119,7 +110,11 @@
     def reader(z, h):
         def load(t):
             a, b = k1_ref[z, t].astype(F32), k2_ref[z, t].astype(F32)
-            return jnp.where(first, a, b) if h == 0 else jnp.where(first, b, a)
+            tile = jnp.where(first, a, b) if h == 0 else jnp.where(first, b, a)
+            if t == 3:
+                tile = tile[: ROWS // 2]
+                tile = jnp.concatenate([tile, rotate(tile, -TAIL)], axis=0)
+            return tile
 
         return cached(load)
 
@@ -170,25 +165,21 @@
             o_ref[a, :, t * LANES : t * LANES + w] = tile[:, :w]
 
 
-def pack(kernel_blocks, density, index):
-    offsets, _, bins = kernel_blocks.shape
-    angles, radii = density.shape
-    groups = -(-offsets * NB // LANES) + density_tiles(angles)[1]
+def pack(mine, yh, kernel_blocks, density):
+    hbm, smem = pl.BlockSpec(memory_space=pltpu.HBM), pl.BlockSpec(memory_space=pltpu.SMEM)
     return pl.pallas_call(
         pack_kernel,
-        grid_spec=pltpu.PrefetchScalarGridSpec(
-            num_scalar_prefetch=1,
-            grid=(1,),
-            in_specs=[
-                pl.BlockSpec((offsets, NR, bins), lambda i, index: (0, index[0], 0)),
-                pl.BlockSpec((angles, radii), lambda i, index: (0, 0)),
-            ],
-            out_specs=pl.BlockSpec((NZ, groups, ROWS, LANES), lambda i, index: (0, 0, 0, 0)),
-        ),
-        out_shape=jax.ShapeDtypeStruct((NZ, groups, ROWS, LANES), BF16),
+        in_specs=[smem, smem, hbm, hbm],
+        out_specs=pl.BlockSpec(memory_space=pltpu.VMEM),
+        out_shape=jax.ShapeDtypeStruct((NZ, 8, ROWS, LANES), BF16),
+        scratch_shapes=[
+            pltpu.VMEM((OFFSETS, NR, NZ * NB), BF16),
+            pltpu.VMEM((VIEWS, NA * NR), BF16),
+            pltpu.SemaphoreType.DMA((2,)),
+        ],
         compiler_params=pltpu.CompilerParams(vmem_limit_bytes=VMEM_BYTES),
         name="pack",
-    )(index, kernel_blocks, density)
+    )(mine, yh, *(pltpu.with_memory_space_constraint(v, pltpu.HBM) for v in (kernel_blocks, density)))
 
 
 def regroup(d):
@@ -204,7 +195,7 @@
 
 
 def project(yh, k1, k2, d):
-    half = 18 * NB
+    half = OFFSETS * NB
     blocks = 2 * NZ * half // (NR * NB)
     width = 2 * NZ * half // NA
     vmem = pl.BlockSpec(memory_space=pltpu.VMEM)
@@ -224,20 +215,18 @@
 
 
 def local(density, kernel_blocks):
-    offsets, angles = kernel_blocks.shape[0], density.shape[1]
-    me = lax.axis_index(ANGLE).astype(jnp.int32).reshape(1)
-    yh = lax.axis_index("yh").astype(jnp.int32).reshape(1)
-    both = lax.all_to_all(pack(kernel_blocks, density[0], me), "z", 0, 0, tiled=True)
-    groups = -(-offsets * NB // LANES)
-    k1 = both[:, :groups]
-    k2 = lax.ppermute(k1, "yh", [(0, 1), (1, 0)])
-    d = regroup(both[:, groups:].transpose(1, 2, 0, 3))
+    yh, yl, x, co = (lax.axis_index(name).astype(jnp.int32) for name in ("yh",) + ANGLE)
+    mine = ((yl ^ yh) * 4 + x) * 2 + co
+    both = lax.all_to_all(pack(mine.reshape(1), yh.reshape(1), kernel_blocks, density), "z", 0, 0, tiled=True)
+    k1 = both[:, :4]
+    k2 = lax.ppermute(k1, ("yh", "yl"), [(0, 3), (1, 2), (2, 1), (3, 0)])
+    d = regroup(both[:, 3:].transpose(1, 2, 0, 3))
     d = lax.all_to_all(d, ANGLE, 0, 0, tiled=True)
-    parts = project(yh, k1, k2, d)
+    parts = project(yh.reshape(1), k1, k2, d)
     parts = lax.all_to_all(parts, ANGLE, 0, 0, tiled=True)
     out = jnp.sum(parts, axis=0).astype(BF16)
     out = lax.all_to_all(out, "z", 0, 0, tiled=True)
-    return out.reshape(NZ, angles, NB).transpose(1, 0, 2).reshape(1, angles, NZ * NB)
+    return out.reshape(NZ, VIEWS, NB).transpose(1, 0, 2).reshape(1, VIEWS, NZ * NB)
 
 
 def solution(mesh):

time: 117 us -> 115 us (0.983)
  the two profiles are of different devices: /device:TPU:1 before, /device:TPU:16 now
where the time goes in v3:
time: 115 us; the launch traced here: 114 us
  blocking collectives  84.1 us (73%)
  Pallas kernels  11.7 us (10%)
  starting transfers between devices  8.12 us (7%)
  waiting for transfers between devices  7.53 us (7%)
  local copies, waits for them, and re-layouts  1.85 us (2%)
    all_to_all x1, blocking collectives, local(): lax.all_to_all(pack(mine.reshape(1), yh.reshape(1), kernel_blocks, densit...  44.1 us
    all_to_all x1, blocking collectives, local(): parts = lax.all_to_all(parts, ANGLE, 0, 0, tiled=True)  21.3 us
    all_to_all x1, blocking collectives, local(): out = lax.all_to_all(out, 'z', 0, 0, tiled=True)  18.7 us
    pallas_call x1, Pallas kernels, project(): pl.pallas_call(main_kernel, in_specs=[pl.BlockSpec(memory_space=pltpu.SME...  8.24 us
    ppermute x1, waiting for transfers between devices, local(): k2 = lax.ppermute(k1, ('yh', 'yl'), [(0, 3), (1, 2), (2, 1), (3, 0)])  7.53 us
    all_to_all x1, starting transfers between devices, local(): d = lax.all_to_all(d, ANGLE, 0, 0, tiled=True)  5.12 us
    ppermute x1, starting transfers between devices, local(): k2 = lax.ppermute(k1, ('yh', 'yl'), [(0, 3), (1, 2), (2, 1), (3, 0)])  3 us
  transfers between devices with their start and end apart: 2, of which 1 were waited for; matrix products, arithmetic and copies ran while one was open for 0% of the time, Pallas kernels for 0%

profile of v3, /device:TPU:16, one launch (start us, length us, event | category | flops | bytes accessed | tf_op | source)
XLA Modules:
  0.0 114.2 jit_solution(1305670407853615250)
XLA Ops:
  0.0 2.1 %pack.1 = bf16[16,8,16,128]{3,2,1,0:T(8,128)(2,1)S(1)} custom-call(s32[1]{0:T(128)} %bitcast.1.mine_ref, s32[1]{0:T(128)} %bitcast.yh_ref, bf16[18,256,384]{2,1,0:T(8,128)(2,1)} %k_hbm.1, bf16[1,36,256]{2,1,0:T(8,128)(2,1)} %d_hbm.1), custom_call_target="tpu_custom_call" | custom-call | tf_op jit(solution)/shard_map/pack/pallas_call | solution.py:170
  2.2 44.1 %all_to_all.21 = bf16[16,8,16,128]{3,2,1,0:T(8,128)(2,1)S(1)} all-to-all(bf16[16,8,16,128]{3,2,1,0:T(8,128)(2,1)S(1)} %pack.1), channel_id=1, replica_groups=mesh['z'=16,'yh'=2,'yl'=2,'x'=4,'co'=2] {'z'}, dimensions={0} | all-to-all | bytes 1048576 | tf_op jit(solution)/shard_map/all_to_all | solution.py:220
  46.3 0.1 copy.8.d_ref
  46.4 1.3 %regroup.1 = bf16[16,5,16,128]{3,2,1,0:T(8,128)(2,1)} custom-call(bf16[5,16,16,128]{3,2,1,0:T(8,128)(2,1)S(1)} %copy.8.d_ref), custom_call_target="tpu_custom_call" | custom-call | tf_op jit(solution)/shard_map/regroup/pallas_call | solution.py:187
  47.7 5.1 %all-to-all-start.1 = ((bf16[16,5,16,128]{3,2,1,0:T(8,128)(2,1)}), bf16[16,5,16,128]{3,2,1,0:T(8,128)(2,1)S(1)}, u32[]{:S(2)}, u32[]{:S(2)}) async-start(bf16[16,5,16,128]{3,2,1,0:T(8,128)(2,1)} %regroup.1), calls=%async_computation.1 | async-start | bytes 655360 | tf_op jit(solution)/shard_map/all_to_all | solution.py:224
  52.8 3.0 %collective-permute-start = (bf16[16,4,16,128]{3,2,1,0:T(8,128)(2,1)S(1)}, bf16[16,4,16,128]{3,2,1,0:T(8,128)(2,1)S(1)}, u32[]{:S(2)}, u32[]{:S(2)}) collective-permute-start(bf16[16,4,16,128]{3,2,1,0:T(8,128)(2,1)S(1)} %slice.8.k1_ref), channel_id=1, source_target_pairs={{0,24},{8,16},{16,8},{24,0},{1,25},{9,17},{17,9},{25,1},{2,26},{10... | collective-permute-start | bytes 786440 | tf_op jit(solution)/shard_map/ppermute | solution.py:222
  55.8 7.5 %collective-permute-done.k2_ref = bf16[16,4,16,128]{3,2,1,0:T(8,128)(2,1)S(1)} collective-permute-done((bf16[16,4,16,128]{3,2,1,0:T(8,128)(2,1)S(1)}, bf16[16,4,16,128]{3,2,1,0:T(8,128)(2,1)S(1)}, u32[]{:S(2)}, u32[]{:S(2)}) %collective-permute-start) | collective-permute-done | bytes 262176 | tf_op jit(solution)/shard_map/ppermute | solution.py:222
  63.4 0.0 all-to-all-done.1.d_ref
  63.4 8.2 %project.1 = f32[16,16,864]{2,1,0:T(8,128)S(1)} custom-call(s32[1]{0:T(128)} %bitcast.yh_ref, bf16[16,4,16,128]{3,2,1,0:T(8,128)(2,1)S(1)} %slice.8.k1_ref, bf16[16,4,16,128]{3,2,1,0:T(8,128)(2,1)S(1)} %collective-permute-done.k2_ref, bf16[16,5,16,128]{3,2,1,0:T(8,128)(2,1)S(1)} %all-to-all-done.1.d_ref), custom_call_target="tpu_custom_call" | custom-call | tf_op jit(solution)/shard_map/project/pallas_call | solution.py:202
  71.6 21.3 %all_to_all.22 = f32[16,16,864]{2,1,0:T(8,128)S(1)} all-to-all(f32[16,16,864]{2,1,0:T(8,128)S(1)} %project.1), channel_id=1, replica_groups=mesh['z'=16,'yh'=2,'yl'=2,'x'=4,'co'=2] {'yl','x','co'}, dimensions={0} | all-to-all | bytes 1769472 | tf_op jit(solution)/shard_map/all_to_all | solution.py:226
  92.9 0.1 reduce_sum.9
  92.9 0.5 broadcast.1
  93.5 0.7 reduce.1
  94.1 0.1 reshape.29
  94.2 18.7 %all_to_all.23 = bf16[16,2,432]{2,1,0:T(2,128)(2,1)S(1)} all-to-all(bf16[16,2,432]{2,1,0:T(2,128)(2,1)S(1)} %reshape.29), channel_id=1, replica_groups=mesh['z'=16,'yh'=2,'yl'=2,'x'=4,'co'=2] {'z'}, dimensions={0} | all-to-all | bytes 55296 | tf_op jit(solution)/shard_map/all_to_all | solution.py:228
  112.9 0.1 reshape.30
  113.1 0.2 reduce
  113.2 0.2 reshape.26
  113.4 0.8 reshape.27
  (3 shorter events, 0.1 us)
Async XLA Ops:
  47.7 15.7 %all-to-all-start.1 = ((bf16[16,5,16,128]{3,2,1,0:T(8,128)(2,1)}), bf16[16,5,16,128]{3,2,1,0:T(8,128)(2,1)S(1)}, u32[]{:S(2)}, u32[]{:S(2)}) async-start(bf16[16,5,16,128]{3,2,1,0:T(8,128)(2,1)} %regroup.1), calls=%async_computation.1 | async-start | bytes 655360 | tf_op jit(solution)/shard_map/all_to_all | solution.py:224
  52.8 10.5 %collective-permute-start = (bf16[16,4,16,128]{3,2,1,0:T(8,128)(2,1)S(1)}, bf16[16,4,16,128]{3,2,1,0:T(8,128)(2,1)S(1)}, u32[]{:S(2)}, u32[]{:S(2)}) collective-permute-start(bf16[16,4,16,128]{3,2,1,0:T(8,128)(2,1)S(1)} %slice.8.k1_ref), channel_id=1, source_target_pairs={{0,24},{8,16},{16,8},{24,0},{1,25},{9,17},{17,9},{25,1},{2,26},{10... | collective-permute-start | bytes 786440 | tf_op jit(solution)/shard_map/ppermute | solution.py:222

commit v4 on v3

--- a/solution.py
+++ b/solution.py
@@ -5,12 +5,14 @@
 from jax.experimental.pallas import tpu as pltpu
 from jax.sharding import Mesh, PartitionSpec as P
 
-CUTS = ("z", "yh")
+Z = ("zp", "zb")
+CUTS = Z + ("yh",)
 ANGLE = ("yl", "x", "co")
 NZ, NA, NR, NB = 16, 16, 16, 24
 OFFSETS, VIEWS = 18, 36
 ROWS, LANES = 16, 128
 TAIL = OFFSETS * NB % LANES
+PART = VIEWS // 2
 F32, BF16 = jnp.float32, jnp.bfloat16
 VMEM_BYTES = 40 << 20
 
@@ -61,23 +63,25 @@
     copies[1].wait()
     low, high = d_ref[:, :LANES].astype(F32), d_ref[:, LANES:].astype(F32)
     halves = jnp.where(swap, high, low), jnp.where(swap, low, high)
-    for n in range(2):
+    rest = []
+    for b in range(2):
+        rows = [half[b * PART : (b + 1) * PART] for half in halves]
         for h in range(2):
-            tile = halves[h][n * ROWS : (n + 1) * ROWS].astype(BF16)
-            for z in range(NZ):
-                o_ref[z, 4 + 2 * n + h] = tile
-    rest = [h[2 * ROWS :] for h in halves]
+            tile = rows[h][:ROWS].astype(BF16)
+            for z in range(b, NZ, 2):
+                o_ref[z, 4 + h] = tile
+        parts = [rotate(rows[q // 2][ROWS:], (1 - q % 2) * LANES // 2) for q in range(4)]
+        rest.append(jnp.concatenate(parts + [jnp.zeros((ROWS - 4 * (PART - ROWS), LANES), F32)], axis=0))
     copies[0].wait()
     readers = [
         cached(lambda t, l=l: k_ref[l, :, t * LANES : (t + 1) * LANES].astype(F32)) for l in range(OFFSETS)
     ]
-    lane = lax.broadcasted_iota(jnp.int32, (ROWS // 2, LANES), 1)
+    lane = lax.broadcasted_iota(jnp.int32, (ROWS, LANES), 1)
     for z in range(NZ):
         tiles = assemble(4, [(readers[l], z * NB, l * NB, NB) for l in range(OFFSETS)])
         for t in range(3):
             o_ref[z, t] = tiles[t].astype(BF16)
-        last = jnp.where(lane < TAIL, tiles[3][: ROWS // 2], rotate(tiles[3][ROWS // 2 :], TAIL))
-        o_ref[z, 3] = jnp.concatenate([last] + rest, axis=0).astype(BF16)
+        o_ref[z, 3] = jnp.where(lane < TAIL, tiles[3], rest[z % 2]).astype(BF16)
 
 
 def regroup_kernel(d_ref, o_ref):
@@ -85,17 +89,18 @@
     lane = lax.broadcasted_iota(jnp.int32, (NZ, LANES), 1)
     masks = [(lane >= p * NR) & (lane < (p + 1) * NR) for p in range(per)]
     out = {}
-    for angle in range(VIEWS):
-        n, i = divmod(angle, ROWS)
+    for angle in range(PART):
         t, p = divmod(angle, per)
-        for h in range(2):
-            tile = d_ref[1 + 2 * n + h, i] if n < 2 else d_ref[0, ROWS // 2 + (VIEWS - 2 * ROWS) * h + i]
-            for k in range(per):
-                turned = rotate(tile, (p - k) * NR)
-                key = (h * per + k, t)
-                out[key] = turned if key not in out else jnp.where(masks[p], turned, out[key])
+        for a in range(NA):
+            if angle < ROWS:
+                tile, at = d_ref[1 + a // per, angle], a % per
+            else:
+                tile, at = d_ref[0, a // 4 * (PART - ROWS) + angle - ROWS], per // 2 + a % 4
+            turned = rotate(tile, (p - at) * NR)
+            out[a, t] = turned if (a, t) not in out else jnp.where(masks[p], turned, out[a, t])
     for (a, t), tile in out.items():
-        o_ref[a, t] = tile
+        for b in range(2):
+            o_ref[b * NA + a, t] = tile
 
 
 def main_kernel(yh_ref, k1_ref, k2_ref, d_ref, o_ref, flat, weights, left):
@@ -110,11 +115,7 @@
     def reader(z, h):
         def load(t):
             a, b = k1_ref[z, t].astype(F32), k2_ref[z, t].astype(F32)
-            tile = jnp.where(first, a, b) if h == 0 else jnp.where(first, b, a)
-            if t == 3:
-                tile = tile[: ROWS // 2]
-                tile = jnp.concatenate([tile, rotate(tile, -TAIL)], axis=0)
-            return tile
+            return jnp.where(first, a, b) if h == 0 else jnp.where(first, b, a)
 
         return cached(load)
 
@@ -126,9 +127,14 @@
     for t in range(group):
         flat[t] = tiles[tiles_all - group + t]
 
-    span = width * NR // NB
+    span = PART * NR
     tiles = assemble(
-        blocks * 2, [(cached(lambda t, a=a: d_ref[a, t].astype(F32)), 0, a * span, span) for a in range(NA)]
+        blocks * 2,
+        [
+            (cached(lambda t, n=b * NA + a: d_ref[n, t].astype(F32)), 0, (2 * a + b) * span, span)
+            for a in range(NA)
+            for b in range(2)
+        ],
     )
     for w in range(blocks):
         for t in range(2):
@@ -171,7 +177,7 @@
         pack_kernel,
         in_specs=[smem, smem, hbm, hbm],
         out_specs=pl.BlockSpec(memory_space=pltpu.VMEM),
-        out_shape=jax.ShapeDtypeStruct((NZ, 8, ROWS, LANES), BF16),
+        out_shape=jax.ShapeDtypeStruct((NZ, 6, ROWS, LANES), BF16),
         scratch_shapes=[
             pltpu.VMEM((OFFSETS, NR, NZ * NB), BF16),
             pltpu.VMEM((VIEWS, NA * NR), BF16),
@@ -188,7 +194,7 @@
         regroup_kernel,
         in_specs=[vmem],
         out_specs=vmem,
-        out_shape=jax.ShapeDtypeStruct((NA, d.shape[0], NZ, LANES), BF16),
+        out_shape=jax.ShapeDtypeStruct((2 * NA, d.shape[0], NZ, LANES), BF16),
         compiler_params=pltpu.CompilerParams(vmem_limit_bytes=VMEM_BYTES),
         name="regroup",
     )(d)
@@ -217,20 +223,20 @@
 def local(density, kernel_blocks):
     yh, yl, x, co = (lax.axis_index(name).astype(jnp.int32) for name in ("yh",) + ANGLE)
     mine = ((yl ^ yh) * 4 + x) * 2 + co
-    both = lax.all_to_all(pack(mine.reshape(1), yh.reshape(1), kernel_blocks, density), "z", 0, 0, tiled=True)
+    both = lax.all_to_all(pack(mine.reshape(1), yh.reshape(1), kernel_blocks, density), Z, 0, 0, tiled=True)
     k1 = both[:, :4]
     k2 = lax.ppermute(k1, ("yh", "yl"), [(0, 3), (1, 2), (2, 1), (3, 0)])
     d = regroup(both[:, 3:].transpose(1, 2, 0, 3))
-    d = lax.all_to_all(d, ANGLE, 0, 0, tiled=True)
+    d = lax.all_to_all(d, ("zb",) + ANGLE, 0, 0, tiled=True)
     parts = project(yh.reshape(1), k1, k2, d)
     parts = lax.all_to_all(parts, ANGLE, 0, 0, tiled=True)
     out = jnp.sum(parts, axis=0).astype(BF16)
-    out = lax.all_to_all(out, "z", 0, 0, tiled=True)
+    out = lax.all_to_all(out, Z, 0, 0, tiled=True)
     return out.reshape(NZ, VIEWS, NB).transpose(1, 0, 2).reshape(1, VIEWS, NZ * NB)
 
 
 def solution(mesh):
-    own = Mesh(mesh.devices.reshape(16, 2, 2, 4, 2), CUTS + ANGLE)
+    own = Mesh(mesh.devices.reshape(8, 2, 2, 2, 4, 2), CUTS + ANGLE)
     return jax.shard_map(
         local,
         mesh=own,

time: 115 us -> 107 us (0.930)
  blocking collectives: 84.1 us -> 79.4 us
  Pallas kernels: 11.7 us -> 8.64 us
    all_to_all x1, blocking collectives: 44.1 us -> 38.8 us  [local(): lax.all_to_all(pack(mine.reshape(1), yh.reshape(1), kernel_blocks, densit...]
    pallas_call x1, Pallas kernels: 8.24 us -> 6.22 us  [project(): pl.pallas_call(main_kernel, in_specs=[pl.BlockSpec(memory_space=pltpu.SME...]
where the time goes in v4:
time: 107 us
  blocking collectives  79.4 us (74%)
  Pallas kernels  8.64 us (8%)
  starting transfers between devices  8.28 us (8%)
  waiting for transfers between devices  7.5 us (7%)
  local copies, waits for them, and re-layouts  1.8 us (2%)
    all_to_all x1, blocking collectives, local(): lax.all_to_all(pack(mine.reshape(1), yh.reshape(1), kernel_blocks, densit...  38.8 us
    all_to_all x1, blocking collectives, local(): parts = lax.all_to_all(parts, ANGLE, 0, 0, tiled=True)  21.3 us
    all_to_all x1, blocking collectives, local(): out = lax.all_to_all(out, Z, 0, 0, tiled=True)  19.4 us
    ppermute x1, waiting for transfers between devices, local(): k2 = lax.ppermute(k1, ('yh', 'yl'), [(0, 3), (1, 2), (2, 1), (3, 0)])  7.5 us
    pallas_call x1, Pallas kernels, project(): pl.pallas_call(main_kernel, in_specs=[pl.BlockSpec(memory_space=pltpu.SME...  6.22 us
    all_to_all x1, starting transfers between devices, local(): d = lax.all_to_all(d, ('zb',) + ANGLE, 0, 0, tiled=True)  5.41 us
    ppermute x1, starting transfers between devices, local(): k2 = lax.ppermute(k1, ('yh', 'yl'), [(0, 3), (1, 2), (2, 1), (3, 0)])  2.87 us
  transfers between devices with their start and end apart: 2, of which 1 were waited for; matrix products, arithmetic and copies ran while one was open for 0% of the time, Pallas kernels for 0%

profile of v4, /device:TPU:16, one launch (start us, length us, event | category | flops | bytes accessed | tf_op | source)
XLA Modules:
  0.0 106.6 jit_solution(4014748665214416490)
XLA Ops:
  0.0 1.3 %pack.1 = bf16[16,6,16,128]{3,2,1,0:T(8,128)(2,1)S(1)} custom-call(s32[1]{0:T(128)} %bitcast.1.mine_ref, s32[1]{0:T(128)} %bitcast.yh_ref, bf16[18,256,384]{2,1,0:T(8,128)(2,1)} %k_hbm.1, bf16[1,36,256]{2,1,0:T(8,128)(2,1)} %d_hbm.1), custom_call_target="tpu_custom_call" | custom-call | tf_op jit(solution)/shard_map/pack/pallas_call | solution.py:176
  1.4 38.8 %all_to_all.21 = bf16[16,6,16,128]{3,2,1,0:T(8,128)(2,1)S(1)} all-to-all(bf16[16,6,16,128]{3,2,1,0:T(8,128)(2,1)S(1)} %pack.1), channel_id=1, replica_groups=mesh['zp'=8,'zb'=2,'yh'=2,'yl'=2,'x'=4,'co'=2] {'zp','zb'}, dimensions={0} | all-to-all | bytes 786432 | tf_op jit(solution)/shard_map/all_to_all | solution.py:226
  40.1 0.1 copy.8.d_ref
  40.2 1.1 %regroup.1 = bf16[32,3,16,128]{3,2,1,0:T(8,128)(2,1)} custom-call(bf16[3,16,16,128]{3,2,1,0:T(8,128)(2,1)S(1)} %copy.8.d_ref), custom_call_target="tpu_custom_call" | custom-call | tf_op jit(solution)/shard_map/regroup/pallas_call | solution.py:193
  41.3 5.4 %all-to-all-start.1 = ((bf16[32,3,16,128]{3,2,1,0:T(8,128)(2,1)}), bf16[32,3,16,128]{3,2,1,0:T(8,128)(2,1)S(1)}, u32[]{:S(2)}, u32[]{:S(2)}) async-start(bf16[32,3,16,128]{3,2,1,0:T(8,128)(2,1)} %regroup.1), calls=%async_computation.1 | async-start | bytes 786432 | tf_op jit(solution)/shard_map/all_to_all | solution.py:230
  46.7 2.9 %collective-permute-start = (bf16[16,4,16,128]{3,2,1,0:T(8,128)(2,1)S(1)}, bf16[16,4,16,128]{3,2,1,0:T(8,128)(2,1)S(1)}, u32[]{:S(2)}, u32[]{:S(2)}) collective-permute-start(bf16[16,4,16,128]{3,2,1,0:T(8,128)(2,1)S(1)} %slice.8.k1_ref), channel_id=1, source_target_pairs={{0,24},{8,16},{16,8},{24,0},{1,25},{9,17},{17,9},{25,1},{2,26},{10... | collective-permute-start | bytes 786440 | tf_op jit(solution)/shard_map/ppermute | solution.py:228
  49.6 7.5 %collective-permute-done.k2_ref = bf16[16,4,16,128]{3,2,1,0:T(8,128)(2,1)S(1)} collective-permute-done((bf16[16,4,16,128]{3,2,1,0:T(8,128)(2,1)S(1)}, bf16[16,4,16,128]{3,2,1,0:T(8,128)(2,1)S(1)}, u32[]{:S(2)}, u32[]{:S(2)}) %collective-permute-start) | collective-permute-done | bytes 262176 | tf_op jit(solution)/shard_map/ppermute | solution.py:228
  57.1 0.0 all-to-all-done.1.d_ref
  57.1 6.2 %project.1 = f32[16,16,864]{2,1,0:T(8,128)S(1)} custom-call(s32[1]{0:T(128)} %bitcast.yh_ref, bf16[16,4,16,128]{3,2,1,0:T(8,128)(2,1)S(1)} %slice.8.k1_ref, bf16[16,4,16,128]{3,2,1,0:T(8,128)(2,1)S(1)} %collective-permute-done.k2_ref, bf16[32,3,16,128]{3,2,1,0:T(8,128)(2,1)S(1)} %all-to-all-done.1.d_ref), custom_call_target="tpu_custom_call" | custom-call | tf_op jit(solution)/shard_map/project/pallas_call | solution.py:208
  63.3 21.3 %all_to_all.22 = f32[16,16,864]{2,1,0:T(8,128)S(1)} all-to-all(f32[16,16,864]{2,1,0:T(8,128)S(1)} %project.1), channel_id=1, replica_groups=mesh['zp'=8,'zb'=2,'yh'=2,'yl'=2,'x'=4,'co'=2] {'yl','x','co'}, dimensions={0} | all-to-all | bytes 1769472 | tf_op jit(solution)/shard_map/all_to_all | solution.py:232
  84.6 0.1 reduce_sum.9
  84.7 0.5 broadcast.1
  85.2 0.7 reduce.1
  85.8 0.1 reshape.29
  86.0 19.4 %all_to_all.23 = bf16[16,2,432]{2,1,0:T(2,128)(2,1)S(1)} all-to-all(bf16[16,2,432]{2,1,0:T(2,128)(2,1)S(1)} %reshape.29), channel_id=1, replica_groups=mesh['zp'=8,'zb'=2,'yh'=2,'yl'=2,'x'=4,'co'=2] {'zp','zb'}, dimensions={0} | all-to-all | bytes 55296 | tf_op jit(solution)/shard_map/all_to_all | solution.py:234
  105.3 0.1 reshape.30
  105.5 0.2 reduce
  105.6 0.2 reshape.26
  105.8 0.8 reshape.27
  (3 shorter events, 0.1 us)
Async XLA Ops:
  41.3 15.8 %all-to-all-start.1 = ((bf16[32,3,16,128]{3,2,1,0:T(8,128)(2,1)}), bf16[32,3,16,128]{3,2,1,0:T(8,128)(2,1)S(1)}, u32[]{:S(2)}, u32[]{:S(2)}) async-start(bf16[32,3,16,128]{3,2,1,0:T(8,128)(2,1)} %regroup.1), calls=%async_computation.1 | async-start | bytes 786432 | tf_op jit(solution)/shard_map/all_to_all | solution.py:230
  46.7 10.4 %collective-permute-start = (bf16[16,4,16,128]{3,2,1,0:T(8,128)(2,1)S(1)}, bf16[16,4,16,128]{3,2,1,0:T(8,128)(2,1)S(1)}, u32[]{:S(2)}, u32[]{:S(2)}) collective-permute-start(bf16[16,4,16,128]{3,2,1,0:T(8,128)(2,1)S(1)} %slice.8.k1_ref), channel_id=1, source_target_pairs={{0,24},{8,16},{16,8},{24,0},{1,25},{9,17},{17,9},{25,1},{2,26},{10... | collective-permute-start | bytes 786440 | tf_op jit(solution)/shard_map/ppermute | solution.py:228

commit v5 on v4

--- a/solution.py
+++ b/solution.py
@@ -84,7 +84,7 @@
         o_ref[z, 3] = jnp.where(lane < TAIL, tiles[3], rest[z % 2]).astype(BF16)
 
 
-def regroup_kernel(d_ref, o_ref):
+def regroup_kernel(k_ref, d_ref, o_ref, swap_ref):
     per = LANES // NR
     lane = lax.broadcasted_iota(jnp.int32, (NZ, LANES), 1)
     masks = [(lane >= p * NR) & (lane < (p + 1) * NR) for p in range(per)]
@@ -101,20 +101,28 @@
     for (a, t), tile in out.items():
         for b in range(2):
             o_ref[b * NA + a, t] = tile
-
-
-def main_kernel(yh_ref, k1_ref, k2_ref, d_ref, o_ref, flat, weights, left):
+    for z in range(NZ):
+        for t in range(3):
+            swap_ref[z * 3 + t] = k_ref[z, t]
+    for z in range(0, NZ, 2):
+        swap_ref[NZ * 3 + z // 2] = jnp.where(lane < TAIL, k_ref[z, 3], rotate(k_ref[z + 1, 3], TAIL))
+
+
+def main_kernel(yh_ref, co_ref, k1_ref, k2_ref, d_ref, own_ref, other_ref, flat, weights, left):
     half = OFFSETS * NB
     group = NR * NB // LANES
     tiles_all = 2 * NZ * half // LANES
     blocks = tiles_all // group
-    width = o_ref.shape[2]
+    width = own_ref.shape[2]
     lane = lax.broadcasted_iota(jnp.int32, (ROWS, LANES), 1)
     first = yh_ref[0] == 0
 
     def reader(z, h):
         def load(t):
-            a, b = k1_ref[z, t].astype(F32), k2_ref[z, t].astype(F32)
+            a = k1_ref[z, t].astype(F32)
+            b = k2_ref[z * 3 + t if t < 3 else NZ * 3 + z // 2].astype(F32)
+            if t == 3 and z % 2:
+                b = rotate(b, -TAIL)
             return jnp.where(first, a, b) if h == 0 else jnp.where(first, b, a)
 
         return cached(load)
@@ -164,11 +172,15 @@
     def out_tile(t):
         return acc[(t // group) * NZ : (t // group + 1) * NZ, (t % group) * LANES : (t % group + 1) * LANES]
 
-    for a in range(NA):
-        tiles = assemble(-(-width // LANES), [(out_tile, a * width, 0, width)])
-        for t, tile in enumerate(tiles):
+    one = co_ref[0] == 1
+    count = -(-width // LANES)
+    for n in range(NA // 2):
+        pair = [assemble(count, [(out_tile, a * width, 0, width)]) for a in (2 * n, 2 * n + 1)]
+        for t in range(count):
             w = min(LANES, width - t * LANES)
-            o_ref[a, :, t * LANES : t * LANES + w] = tile[:, :w]
+            even, odd = (p[t][:, :w] for p in pair)
+            own_ref[n, :, t * LANES : t * LANES + w] = jnp.where(one, odd, even)
+            other_ref[n, :, t * LANES : t * LANES + w] = jnp.where(one, even, odd)
 
 
 def pack(mine, yh, kernel_blocks, density):
@@ -188,28 +200,32 @@
     )(mine, yh, *(pltpu.with_memory_space_constraint(v, pltpu.HBM) for v in (kernel_blocks, density)))
 
 
-def regroup(d):
+def regroup(both):
     vmem = pl.BlockSpec(memory_space=pltpu.VMEM)
+    d = both[:, 3:].transpose(1, 2, 0, 3)
     return pl.pallas_call(
         regroup_kernel,
-        in_specs=[vmem],
-        out_specs=vmem,
-        out_shape=jax.ShapeDtypeStruct((2 * NA, d.shape[0], NZ, LANES), BF16),
+        in_specs=[vmem, vmem],
+        out_specs=[vmem, vmem],
+        out_shape=[
+            jax.ShapeDtypeStruct((2 * NA, d.shape[0], NZ, LANES), BF16),
+            jax.ShapeDtypeStruct((NZ * 3 + NZ // 2, ROWS, LANES), BF16),
+        ],
         compiler_params=pltpu.CompilerParams(vmem_limit_bytes=VMEM_BYTES),
         name="regroup",
-    )(d)
-
-
-def project(yh, k1, k2, d):
+    )(both, d)
+
+
+def project(yh, co, k1, k2, d):
     half = OFFSETS * NB
     blocks = 2 * NZ * half // (NR * NB)
     width = 2 * NZ * half // NA
-    vmem = pl.BlockSpec(memory_space=pltpu.VMEM)
+    smem, vmem = pl.BlockSpec(memory_space=pltpu.SMEM), pl.BlockSpec(memory_space=pltpu.VMEM)
     return pl.pallas_call(
         main_kernel,
-        in_specs=[pl.BlockSpec(memory_space=pltpu.SMEM), vmem, vmem, vmem],
-        out_specs=vmem,
-        out_shape=jax.ShapeDtypeStruct((NA, NZ, width), F32),
+        in_specs=[smem, smem, vmem, vmem, vmem],
+        out_specs=[vmem, vmem],
+        out_shape=[jax.ShapeDtypeStruct((NA // 2, NZ, width), F32)] * 2,
         scratch_shapes=[
             pltpu.VMEM((2 * NZ * half // LANES + NR * NB // LANES, ROWS, LANES), F32),
             pltpu.VMEM((blocks, NR * NR, NR * NB), BF16),
@@ -217,19 +233,19 @@
         ],
         compiler_params=pltpu.CompilerParams(vmem_limit_bytes=VMEM_BYTES),
         name="project",
-    )(yh, k1, k2, d)
+    )(yh, co, k1, k2, d)
 
 
 def local(density, kernel_blocks):
     yh, yl, x, co = (lax.axis_index(name).astype(jnp.int32) for name in ("yh",) + ANGLE)
     mine = ((yl ^ yh) * 4 + x) * 2 + co
     both = lax.all_to_all(pack(mine.reshape(1), yh.reshape(1), kernel_blocks, density), Z, 0, 0, tiled=True)
-    k1 = both[:, :4]
-    k2 = lax.ppermute(k1, ("yh", "yl"), [(0, 3), (1, 2), (2, 1), (3, 0)])
-    d = regroup(both[:, 3:].transpose(1, 2, 0, 3))
+    d, k2 = regroup(both)
+    k2 = lax.ppermute(k2, ("yh", "yl"), [(0, 3), (1, 2), (2, 1), (3, 0)])
     d = lax.all_to_all(d, ("zb",) + ANGLE, 0, 0, tiled=True)
-    parts = project(yh.reshape(1), k1, k2, d)
-    parts = lax.all_to_all(parts, ANGLE, 0, 0, tiled=True)
+    own, other = project(yh.reshape(1), co.reshape(1), both, k2, d)
+    parts = own + lax.ppermute(other, "co", [(0, 1), (1, 0)])
+    parts = lax.all_to_all(parts, ("yl", "x"), 0, 0, tiled=True)
     out = jnp.sum(parts, axis=0).astype(BF16)
     out = lax.all_to_all(out, Z, 0, 0, tiled=True)
     return out.reshape(NZ, VIEWS, NB).transpose(1, 0, 2).reshape(1, VIEWS, NZ * NB)

time: 107 us -> 105 us (0.981)
  blocking collectives: 79.4 us -> 74.1 us
  starting transfers between devices: 8.28 us -> 10.3 us
    all_to_all x1, blocking collectives: 21.3 us -> 16 us  [local(): parts = lax.all_to_all(parts, ('yl', 'x'), 0, 0, tiled=True)]
    ppermute x1 -> x2, starting transfers between devices: 2.87 us -> 4.93 us  [the longest x1 2.87 us: local(): k2 = lax.ppermute(k2, ('yh', 'yl'), [(0, 3), (1, 2), (2, 1), (3, 0)])]
    ppermute x1 -> x2, waiting for transfers between devices: 7.5 us -> 8.44 us  [the longest x1 6.8 us: local(): k2 = lax.ppermute(k2, ('yh', 'yl'), [(0, 3), (1, 2), (2, 1), (3, 0)])]
  transfers between devices with their start and end apart: 2 -> 3, of which waited for: 1 -> 3; matrix products, arithmetic and copies ran while one was open for 0% -> 0% of each run, Pallas kernels for 0% -> 0%
where the time goes in v5:
time: 105 us
  blocking collectives  74.1 us (71%)
  starting transfers between devices  10.3 us (10%)
  Pallas kernels  8.89 us (8%)
  waiting for transfers between devices  8.49 us (8%)
  local copies, waits for them, and re-layouts  1.78 us (2%)
    all_to_all x1, blocking collectives, local(): lax.all_to_all(pack(mine.reshape(1), yh.reshape(1), kernel_blocks, densit...  38.8 us
    all_to_all x1, blocking collectives, local(): out = lax.all_to_all(out, Z, 0, 0, tiled=True)  19.4 us
    all_to_all x1, blocking collectives, local(): parts = lax.all_to_all(parts, ('yl', 'x'), 0, 0, tiled=True)  16 us
    ppermute x1, waiting for transfers between devices, local(): k2 = lax.ppermute(k2, ('yh', 'yl'), [(0, 3), (1, 2), (2, 1), (3, 0)])  6.8 us
    pallas_call x1, Pallas kernels, project(): pl.pallas_call(main_kernel, in_specs=[smem, smem, vmem, vmem, vmem], out_...  6.46 us
    all_to_all x1, starting transfers between devices, local(): d = lax.all_to_all(d, ('zb',) + ANGLE, 0, 0, tiled=True)  5.41 us
    ppermute x1, starting transfers between devices, local(): k2 = lax.ppermute(k2, ('yh', 'yl'), [(0, 3), (1, 2), (2, 1), (3, 0)])  2.87 us
  transfers between devices with their start and end apart: 3, of which 3 were waited for; matrix products, arithmetic and copies ran while one was open for 0% of the time, Pallas kernels for 0%

profile of v5, /device:TPU:16, one launch (start us, length us, event | category | flops | bytes accessed | tf_op | source)
XLA Modules:
  0.0 104.6 jit_solution(8575549342380988341)
XLA Ops:
  0.0 1.3 %pack.1 = bf16[16,6,16,128]{3,2,1,0:T(8,128)(2,1)S(1)} custom-call(s32[1]{0:T(128)} %bitcast.2.mine_ref, s32[1]{0:T(128)} %bitcast.yh_ref, bf16[18,256,384]{2,1,0:T(8,128)(2,1)} %k_hbm.1, bf16[1,36,256]{2,1,0:T(8,128)(2,1)} %d_hbm.1), custom_call_target="tpu_custom_call" | custom-call | tf_op jit(solution)/shard_map/pack/pallas_call | solution.py:188
  1.4 38.8 %all_to_all.21.k_ref.k1_ref = bf16[16,6,16,128]{3,2,1,0:T(8,128)(2,1)S(1)} all-to-all(bf16[16,6,16,128]{3,2,1,0:T(8,128)(2,1)S(1)} %pack.1), channel_id=1, replica_groups=mesh['zp'=8,'zb'=2,'yh'=2,'yl'=2,'x'=4,'co'=2] {'zp','zb'}, dimensions={0} | all-to-all | bytes 786432 | tf_op jit(solution)/shard_map/all_to_all | solution.py:242
  40.1 0.1 copy.8.d_ref
  40.2 1.1 %regroup.1 = (bf16[32,3,16,128]{3,2,1,0:T(8,128)(2,1)}, bf16[56,16,128]{2,1,0:T(8,128)(2,1)S(1)}) custom-call(bf16[16,6,16,128]{3,2,1,0:T(8,128)(2,1)S(1)} %all_to_all.21.k_ref.k1_ref, bf16[3,16,16,128]{3,2,1,0:T(8,128)(2,1)S(1)} %copy.8.d_ref), custom_call_target="tpu_custom_call" | custom-call | tf_op jit(solution)/shard_map/regroup/pallas_call | solution.py:206
  41.3 5.4 %all-to-all-start.1 = ((bf16[32,3,16,128]{3,2,1,0:T(8,128)(2,1)}), bf16[32,3,16,128]{3,2,1,0:T(8,128)(2,1)S(1)}, u32[]{:S(2)}, u32[]{:S(2)}) async-start(bf16[32,3,16,128]{3,2,1,0:T(8,128)(2,1)} %get-tuple-element.10), calls=%async_computation.1 | async-start | bytes 786432 | tf_op jit(solution)/shard_map/all_to_all | solution.py:245
  46.7 2.9 %collective-permute-start = (bf16[56,16,128]{2,1,0:T(8,128)(2,1)S(1)}, bf16[56,16,128]{2,1,0:T(8,128)(2,1)S(1)}, u32[]{:S(2)}, u32[]{:S(2)}) collective-permute-start(bf16[56,16,128]{2,1,0:T(8,128)(2,1)S(1)} %get-tuple-element.9), channel_id=1, source_target_pairs={{0,24},{8,16},{16,8},{24,0},{1,25},{9,17},{17,9},{25,1},{2,26},{10... | collective-permute-start | bytes 688136 | tf_op jit(solution)/shard_map/ppermute | solution.py:244
  49.6 6.8 %collective-permute-done.k2_ref = bf16[56,16,128]{2,1,0:T(8,128)(2,1)S(1)} collective-permute-done((bf16[56,16,128]{2,1,0:T(8,128)(2,1)S(1)}, bf16[56,16,128]{2,1,0:T(8,128)(2,1)S(1)}, u32[]{:S(2)}, u32[]{:S(2)}) %collective-permute-start) | collective-permute-done | bytes 229408 | tf_op jit(solution)/shard_map/ppermute | solution.py:244
  56.4 0.1 all-to-all-done.1.d_ref
  56.4 6.5 %project.1 = (f32[8,16,864]{2,1,0:T(8,128)S(1)}, f32[8,16,864]{2,1,0:T(8,128)S(1)}) custom-call(s32[1]{0:T(128)} %bitcast.yh_ref, s32[1]{0:T(128)} %bitcast.1.co_ref, bf16[16,6,16,128]{3,2,1,0:T(8,128)(2,1)S(1)} %all_to_all.21.k_ref.k1_ref, bf16[56,16,128]{2,1,0:T(8,128)(2,1)S(1)} %collective-permute-done.k2_ref, ...), custom_call_target="tpu_custom_call" | custom-call | tf_op jit(solution)/shard_map/project/pallas_call | solution.py:224
  62.9 2.1 %collective-permute-start.1 = (f32[8,16,864]{2,1,0:T(8,128)S(1)}, f32[8,16,864]{2,1,0:T(8,128)S(1)}, u32[]{:S(2)}, u32[]{:S(2)}) collective-permute-start(f32[8,16,864]{2,1,0:T(8,128)S(1)} %get-tuple-element.12), channel_id=1, source_target_pairs={{0,1},{1,0},{2,3},{3,2},{4,5},{5,4},{6,7},{7,6},{8,9},{9,8},{10,11... | collective-permute-start | bytes 1327112 | tf_op jit(solution)/shard_map/ppermute | solution.py:247
  65.0 1.6 %collective-permute-done.1 = f32[8,16,864]{2,1,0:T(8,128)S(1)} collective-permute-done((f32[8,16,864]{2,1,0:T(8,128)S(1)}, f32[8,16,864]{2,1,0:T(8,128)S(1)}, u32[]{:S(2)}, u32[]{:S(2)}) %collective-permute-start.1) | collective-permute-done | bytes 442400 | tf_op jit(solution)/shard_map/ppermute | solution.py:247
  66.6 0.1 add.11
  66.7 16.0 %all_to_all.22 = f32[8,16,864]{2,1,0:T(8,128)S(1)} all-to-all(f32[8,16,864]{2,1,0:T(8,128)S(1)} %add.11), channel_id=1, replica_groups=mesh['zp'=8,'zb'=2,'yh'=2,'yl'=2,'x'=4,'co'=2] {'yl','x'}, dimensions={0} | all-to-all | bytes 884736 | tf_op jit(solution)/shard_map/all_to_all | solution.py:248
  82.7 0.5 broadcast.1
  83.2 0.7 reduce.1
  83.9 0.1 reshape.33
  84.0 19.4 %all_to_all.23 = bf16[16,2,432]{2,1,0:T(2,128)(2,1)S(1)} all-to-all(bf16[16,2,432]{2,1,0:T(2,128)(2,1)S(1)} %reshape.33), channel_id=1, replica_groups=mesh['zp'=8,'zb'=2,'yh'=2,'yl'=2,'x'=4,'co'=2] {'zp','zb'}, dimensions={0} | all-to-all | bytes 55296 | tf_op jit(solution)/shard_map/all_to_all | solution.py:250
  103.4 0.1 reshape.34
  103.5 0.2 reduce
  103.6 0.2 reshape.30
  103.8 0.8 reshape.31
  (3 shorter events, 0.1 us)
Async XLA Ops:
  41.3 15.1 %all-to-all-start.1 = ((bf16[32,3,16,128]{3,2,1,0:T(8,128)(2,1)}), bf16[32,3,16,128]{3,2,1,0:T(8,128)(2,1)S(1)}, u32[]{:S(2)}, u32[]{:S(2)}) async-start(bf16[32,3,16,128]{3,2,1,0:T(8,128)(2,1)} %get-tuple-element.10), calls=%async_computation.1 | async-start | bytes 786432 | tf_op jit(solution)/shard_map/all_to_all | solution.py:245
  46.7 9.7 %collective-permute-start = (bf16[56,16,128]{2,1,0:T(8,128)(2,1)S(1)}, bf16[56,16,128]{2,1,0:T(8,128)(2,1)S(1)}, u32[]{:S(2)}, u32[]{:S(2)}) collective-permute-start(bf16[56,16,128]{2,1,0:T(8,128)(2,1)S(1)} %get-tuple-element.9), channel_id=1, source_target_pairs={{0,24},{8,16},{16,8},{24,0},{1,25},{9,17},{17,9},{25,1},{2,26},{10... | collective-permute-start | bytes 688136 | tf_op jit(solution)/shard_map/ppermute | solution.py:244
  62.9 3.7 %collective-permute-start.1 = (f32[8,16,864]{2,1,0:T(8,128)S(1)}, f32[8,16,864]{2,1,0:T(8,128)S(1)}, u32[]{:S(2)}, u32[]{:S(2)}) collective-permute-start(f32[8,16,864]{2,1,0:T(8,128)S(1)} %get-tuple-element.12), channel_id=1, source_target_pairs={{0,1},{1,0},{2,3},{3,2},{4,5},{5,4},{6,7},{7,6},{8,9},{9,8},{10,11... | collective-permute-start | bytes 1327112 | tf_op jit(solution)/shard_map/ppermute | solution.py:247

commit v6 on v5

--- a/solution.py
+++ b/solution.py
@@ -108,7 +108,7 @@
         swap_ref[NZ * 3 + z // 2] = jnp.where(lane < TAIL, k_ref[z, 3], rotate(k_ref[z + 1, 3], TAIL))
 
 
-def main_kernel(yh_ref, co_ref, k1_ref, k2_ref, d_ref, own_ref, other_ref, flat, weights, left):
+def main_kernel(yh_ref, co_ref, k1_ref, k2_ref, d_ref, own_ref, other_ref, flat, weights, paired, left):
     half = OFFSETS * NB
     group = NR * NB // LANES
     tiles_all = 2 * NZ * half // LANES
@@ -160,18 +160,24 @@
                 outs = [jnp.where(lane >= rem, turned[t + 1], turned[t]) for t in range(group)]
             else:
                 outs = [flat[base + t] for t in range(group)]
-            for t in range(group):
-                weights[block, j * NR : (j + 1) * NR, t * LANES : (t + 1) * LANES] = outs[t].astype(BF16)
+            rows = slice(block * NR * NR + j * NR, block * NR * NR + (j + 1) * NR)
+            for t in range(group - 1):
+                weights[rows, t * LANES : (t + 1) * LANES] = outs[t].astype(BF16)
+            pair, side = divmod(block, 2)
+            rows = slice(pair * NR * NR + j * NR, pair * NR * NR + (j + 1) * NR)
+            paired[rows, side * LANES : (side + 1) * LANES] = outs[group - 1].astype(BF16)
     lhs = [left[(blocks - c) * NZ : (2 * blocks - c) * NZ, :] for c in range(blocks)]
-    acc = jnp.dot(
-        jnp.concatenate(lhs, axis=1),
-        weights[...].reshape(blocks * NR * NR, NR * NB),
-        preferred_element_type=F32,
-    )
-
-    def out_tile(t):
-        return acc[(t // group) * NZ : (t // group + 1) * NZ, (t % group) * LANES : (t % group + 1) * LANES]
-
+    acc = jnp.dot(jnp.concatenate(lhs, axis=1), weights[...], preferred_element_type=F32)
+    last = jnp.dot(jnp.concatenate(lhs[::2], axis=1), paired[...], preferred_element_type=F32)
+
+    def tile_of(t):
+        u, t = divmod(t, group)
+        if t < group - 1:
+            return acc[u * NZ : (u + 1) * NZ, t * LANES : (t + 1) * LANES]
+        before = (u - 1) % blocks
+        return last[u * NZ : (u + 1) * NZ, :LANES] + last[before * NZ : (before + 1) * NZ, LANES:]
+
+    out_tile = cached(tile_of)
     one = co_ref[0] == 1
     count = -(-width // LANES)
     for n in range(NA // 2):
@@ -183,6 +189,18 @@
             other_ref[n, :, t * LANES : t * LANES + w] = jnp.where(one, even, odd)
 
 
+def fold_kernel(p_ref, o_ref, rows):
+    width = p_ref.shape[2]
+    rows[...] = jnp.zeros_like(rows)
+    for t in range(-(-width // LANES)):
+        w = min(LANES, width - t * LANES)
+        tile = p_ref[0, :, t * LANES : t * LANES + w]
+        for n in range(1, p_ref.shape[0]):
+            tile = tile + p_ref[n, :, t * LANES : t * LANES + w]
+        rows[:, t, :w] = tile
+    o_ref[...] = rows[...].astype(BF16)
+
+
 def pack(mine, yh, kernel_blocks, density):
     hbm, smem = pl.BlockSpec(memory_space=pltpu.HBM), pl.BlockSpec(memory_space=pltpu.SMEM)
     return pl.pallas_call(
@@ -228,12 +246,26 @@
         out_shape=[jax.ShapeDtypeStruct((NA // 2, NZ, width), F32)] * 2,
         scratch_shapes=[
             pltpu.VMEM((2 * NZ * half // LANES + NR * NB // LANES, ROWS, LANES), F32),
-            pltpu.VMEM((blocks, NR * NR, NR * NB), BF16),
+            pltpu.VMEM((blocks * NR * NR, 2 * LANES), BF16),
+            pltpu.VMEM((blocks // 2 * NR * NR, 2 * LANES), BF16),
             pltpu.VMEM((2 * blocks * NZ, NR * NR), BF16),
         ],
         compiler_params=pltpu.CompilerParams(vmem_limit_bytes=VMEM_BYTES),
         name="project",
     )(yh, co, k1, k2, d)
+
+
+def fold(parts):
+    vmem = pl.BlockSpec(memory_space=pltpu.VMEM)
+    return pl.pallas_call(
+        fold_kernel,
+        in_specs=[vmem],
+        out_specs=vmem,
+        out_shape=jax.ShapeDtypeStruct((NZ, 8, LANES), BF16),
+        scratch_shapes=[pltpu.VMEM((NZ, 8, LANES), F32)],
+        compiler_params=pltpu.CompilerParams(vmem_limit_bytes=VMEM_BYTES),
+        name="fold",
+    )(parts)
 
 
 def local(density, kernel_blocks):
@@ -246,9 +278,9 @@
     own, other = project(yh.reshape(1), co.reshape(1), both, k2, d)
     parts = own + lax.ppermute(other, "co", [(0, 1), (1, 0)])
     parts = lax.all_to_all(parts, ("yl", "x"), 0, 0, tiled=True)
-    out = jnp.sum(parts, axis=0).astype(BF16)
-    out = lax.all_to_all(out, Z, 0, 0, tiled=True)
-    return out.reshape(NZ, VIEWS, NB).transpose(1, 0, 2).reshape(1, VIEWS, NZ * NB)
+    out = lax.all_to_all(fold(parts), Z, 0, 0, tiled=True)
+    out = out.reshape(NZ, -1)[:, : VIEWS * NB].reshape(NZ, VIEWS, NB)
+    return out.transpose(1, 0, 2).reshape(1, VIEWS, NZ * NB)
 
 
 def solution(mesh):

time: 105 us -> 102 us (0.971)
  Pallas kernels: 8.89 us -> 7.74 us
    pallas_call x1, Pallas kernels: 6.46 us -> 5.25 us  [project(): pl.pallas_call(main_kernel, in_specs=[smem, smem, vmem, vmem, vmem], out_...]
where the time goes in v6:
time: 102 us
  blocking collectives  74.1 us (73%)
  starting transfers between devices  10.3 us (10%)
  waiting for transfers between devices  8.5 us (8%)
  Pallas kernels  7.74 us (8%)
  local copies, waits for them, and re-layouts  1.07 us (1%)
    all_to_all x1, blocking collectives, local(): lax.all_to_all(pack(mine.reshape(1), yh.reshape(1), kernel_blocks, densit...  38.8 us
    all_to_all x1, blocking collectives, local(): out = lax.all_to_all(fold(parts), Z, 0, 0, tiled=True)  19.4 us
    all_to_all x1, blocking collectives, local(): parts = lax.all_to_all(parts, ('yl', 'x'), 0, 0, tiled=True)  16 us
    ppermute x1, waiting for transfers between devices, local(): k2 = lax.ppermute(k2, ('yh', 'yl'), [(0, 3), (1, 2), (2, 1), (3, 0)])  6.8 us
    all_to_all x1, starting transfers between devices, local(): d = lax.all_to_all(d, ('zb',) + ANGLE, 0, 0, tiled=True)  5.41 us
    pallas_call x1, Pallas kernels, project(): pl.pallas_call(main_kernel, in_specs=[smem, smem, vmem, vmem, vmem], out_...  5.25 us
    ppermute x1, starting transfers between devices, local(): k2 = lax.ppermute(k2, ('yh', 'yl'), [(0, 3), (1, 2), (2, 1), (3, 0)])  2.87 us
    ppermute x1, starting transfers between devices, local(): parts = own + lax.ppermute(other, 'co', [(0, 1), (1, 0)])  2.06 us
  transfers between devices with their start and end apart: 3, of which 3 were waited for; matrix products, arithmetic and copies ran while one was open for 0% of the time, Pallas kernels for 0%

profile of v6, /device:TPU:16, one launch (start us, length us, event | category | flops | bytes accessed | tf_op | source)
XLA Modules:
  0.0 101.9 jit_solution(9888745411710290947)
XLA Ops:
  0.0 1.3 %pack.1 = bf16[16,6,16,128]{3,2,1,0:T(8,128)(2,1)S(1)} custom-call(s32[1]{0:T(128)} %bitcast.2.mine_ref, s32[1]{0:T(128)} %bitcast.yh_ref, bf16[18,256,384]{2,1,0:T(8,128)(2,1)} %k_hbm.1, bf16[1,36,256]{2,1,0:T(8,128)(2,1)} %d_hbm.1), custom_call_target="tpu_custom_call" | custom-call | tf_op jit(solution)/shard_map/pack/pallas_call | solution.py:206
  1.4 38.8 %all_to_all.20.k_ref.k1_ref = bf16[16,6,16,128]{3,2,1,0:T(8,128)(2,1)S(1)} all-to-all(bf16[16,6,16,128]{3,2,1,0:T(8,128)(2,1)S(1)} %pack.1), channel_id=1, replica_groups=mesh['zp'=8,'zb'=2,'yh'=2,'yl'=2,'x'=4,'co'=2] {'zp','zb'}, dimensions={0} | all-to-all | bytes 786432 | tf_op jit(solution)/shard_map/all_to_all | solution.py:274
  40.1 0.1 copy.5.d_ref
  40.2 1.1 %regroup.1 = (bf16[32,3,16,128]{3,2,1,0:T(8,128)(2,1)}, bf16[56,16,128]{2,1,0:T(8,128)(2,1)S(1)}) custom-call(bf16[16,6,16,128]{3,2,1,0:T(8,128)(2,1)S(1)} %all_to_all.20.k_ref.k1_ref, bf16[3,16,16,128]{3,2,1,0:T(8,128)(2,1)S(1)} %copy.5.d_ref), custom_call_target="tpu_custom_call" | custom-call | tf_op jit(solution)/shard_map/regroup/pallas_call | solution.py:224
  41.3 5.4 %all-to-all-start.1 = ((bf16[32,3,16,128]{3,2,1,0:T(8,128)(2,1)}), bf16[32,3,16,128]{3,2,1,0:T(8,128)(2,1)S(1)}, u32[]{:S(2)}, u32[]{:S(2)}) async-start(bf16[32,3,16,128]{3,2,1,0:T(8,128)(2,1)} %get-tuple-element.10), calls=%async_computation.1 | async-start | bytes 786432 | tf_op jit(solution)/shard_map/all_to_all | solution.py:277
  46.7 2.9 %collective-permute-start = (bf16[56,16,128]{2,1,0:T(8,128)(2,1)S(1)}, bf16[56,16,128]{2,1,0:T(8,128)(2,1)S(1)}, u32[]{:S(2)}, u32[]{:S(2)}) collective-permute-start(bf16[56,16,128]{2,1,0:T(8,128)(2,1)S(1)} %get-tuple-element.9), channel_id=1, source_target_pairs={{0,24},{8,16},{16,8},{24,0},{1,25},{9,17},{17,9},{25,1},{2,26},{10... | collective-permute-start | bytes 688136 | tf_op jit(solution)/shard_map/ppermute | solution.py:276
  49.6 6.8 %collective-permute-done.k2_ref = bf16[56,16,128]{2,1,0:T(8,128)(2,1)S(1)} collective-permute-done((bf16[56,16,128]{2,1,0:T(8,128)(2,1)S(1)}, bf16[56,16,128]{2,1,0:T(8,128)(2,1)S(1)}, u32[]{:S(2)}, u32[]{:S(2)}) %collective-permute-start) | collective-permute-done | bytes 229408 | tf_op jit(solution)/shard_map/ppermute | solution.py:276
  56.4 0.1 all-to-all-done.1.d_ref
  56.4 5.2 %project.1 = (f32[8,16,864]{2,1,0:T(8,128)S(1)}, f32[8,16,864]{2,1,0:T(8,128)S(1)}) custom-call(s32[1]{0:T(128)} %bitcast.yh_ref, s32[1]{0:T(128)} %bitcast.1.co_ref, bf16[16,6,16,128]{3,2,1,0:T(8,128)(2,1)S(1)} %all_to_all.20.k_ref.k1_ref, bf16[56,16,128]{2,1,0:T(8,128)(2,1)S(1)} %collective-permute-done.k2_ref, ...), custom_call_target="tpu_custom_call" | custom-call | tf_op jit(solution)/shard_map/project/pallas_call | solution.py:242
  61.7 2.1 %collective-permute-start.1 = (f32[8,16,864]{2,1,0:T(8,128)S(1)}, f32[8,16,864]{2,1,0:T(8,128)S(1)}, u32[]{:S(2)}, u32[]{:S(2)}) collective-permute-start(f32[8,16,864]{2,1,0:T(8,128)S(1)} %get-tuple-element.12), channel_id=1, source_target_pairs={{0,1},{1,0},{2,3},{3,2},{4,5},{5,4},{6,7},{7,6},{8,9},{9,8},{10,11... | collective-permute-start | bytes 1327112 | tf_op jit(solution)/shard_map/ppermute | solution.py:279
  63.8 1.6 %collective-permute-done.1 = f32[8,16,864]{2,1,0:T(8,128)S(1)} collective-permute-done((f32[8,16,864]{2,1,0:T(8,128)S(1)}, f32[8,16,864]{2,1,0:T(8,128)S(1)}, u32[]{:S(2)}, u32[]{:S(2)}) %collective-permute-start.1) | collective-permute-done | bytes 442400 | tf_op jit(solution)/shard_map/ppermute | solution.py:279
  65.4 0.1 add.11
  65.5 16.0 %all_to_all.21.p_ref = f32[8,16,864]{2,1,0:T(8,128)S(1)} all-to-all(f32[8,16,864]{2,1,0:T(8,128)S(1)} %add.11), channel_id=1, replica_groups=mesh['zp'=8,'zb'=2,'yh'=2,'yl'=2,'x'=4,'co'=2] {'yl','x'}, dimensions={0} | all-to-all | bytes 884736 | tf_op jit(solution)/shard_map/all_to_all | solution.py:280
  81.5 0.1 fold.1
  81.5 19.4 %all_to_all.22 = bf16[16,8,128]{2,1,0:T(8,128)(2,1)S(1)} all-to-all(bf16[16,8,128]{2,1,0:T(8,128)(2,1)S(1)} %fold.1), channel_id=1, replica_groups=mesh['zp'=8,'zb'=2,'yh'=2,'yl'=2,'x'=4,'co'=2] {'zp','zb'}, dimensions={0} | all-to-all | bytes 65536 | tf_op jit(solution)/shard_map/all_to_all | solution.py:281
  100.9 0.2 reshape.23
  101.1 0.8 reshape.24
  (4 shorter events, 0.0 us)
Async XLA Ops:
  41.3 15.1 %all-to-all-start.1 = ((bf16[32,3,16,128]{3,2,1,0:T(8,128)(2,1)}), bf16[32,3,16,128]{3,2,1,0:T(8,128)(2,1)S(1)}, u32[]{:S(2)}, u32[]{:S(2)}) async-start(bf16[32,3,16,128]{3,2,1,0:T(8,128)(2,1)} %get-tuple-element.10), calls=%async_computation.1 | async-start | bytes 786432 | tf_op jit(solution)/shard_map/all_to_all | solution.py:277
  46.7 9.7 %collective-permute-start = (bf16[56,16,128]{2,1,0:T(8,128)(2,1)S(1)}, bf16[56,16,128]{2,1,0:T(8,128)(2,1)S(1)}, u32[]{:S(2)}, u32[]{:S(2)}) collective-permute-start(bf16[56,16,128]{2,1,0:T(8,128)(2,1)S(1)} %get-tuple-element.9), channel_id=1, source_target_pairs={{0,24},{8,16},{16,8},{24,0},{1,25},{9,17},{17,9},{25,1},{2,26},{10... | collective-permute-start | bytes 688136 | tf_op jit(solution)/shard_map/ppermute | solution.py:276
  61.7 3.7 %collective-permute-start.1 = (f32[8,16,864]{2,1,0:T(8,128)S(1)}, f32[8,16,864]{2,1,0:T(8,128)S(1)}, u32[]{:S(2)}, u32[]{:S(2)}) collective-permute-start(f32[8,16,864]{2,1,0:T(8,128)S(1)} %get-tuple-element.12), channel_id=1, source_target_pairs={{0,1},{1,0},{2,3},{3,2},{4,5},{5,4},{6,7},{7,6},{8,9},{9,8},{10,11... | collective-permute-start | bytes 1327112 | tf_op jit(solution)/shard_map/ppermute | solution.py:279

commit v7 on v6

--- a/solution.py
+++ b/solution.py
@@ -22,8 +22,8 @@
     return tile if shift == 0 else pltpu.roll(tile, shift, 1)
 
 
-def assemble(count, pieces):
-    lane = lax.broadcasted_iota(jnp.int32, (ROWS, LANES), 1)
+def assemble(count, pieces, rows=ROWS):
+    lane = lax.broadcasted_iota(jnp.int32, (rows, LANES), 1)
     tiles, cache = [None] * count, {}
     for n, (get, src, dst, width) in enumerate(pieces):
         while width > 0:
@@ -190,15 +190,27 @@
 
 
 def fold_kernel(p_ref, o_ref, rows):
-    width = p_ref.shape[2]
-    rows[...] = jnp.zeros_like(rows)
-    for t in range(-(-width // LANES)):
-        w = min(LANES, width - t * LANES)
+    def load(t):
+        w = min(LANES, p_ref.shape[2] - t * LANES)
         tile = p_ref[0, :, t * LANES : t * LANES + w]
         for n in range(1, p_ref.shape[0]):
             tile = tile + p_ref[n, :, t * LANES : t * LANES + w]
-        rows[:, t, :w] = tile
+        return tile if w == LANES else jnp.concatenate([tile, jnp.zeros((NZ, LANES - w), F32)], axis=1)
+
+    get = cached(load)
+    for i in range(8):
+        pieces = [(get, v * NB, v // 8 * NB, NB) for v in range(i, VIEWS, 8)]
+        rows[:, i, :] = assemble(1, pieces)[0]
     o_ref[...] = rows[...].astype(BF16)
+
+
+def place_kernel(t_ref, o_ref):
+    readers = [cached(lambda t, z=z: t_ref[z].astype(F32)) for z in range(NZ)]
+    for first in range(0, VIEWS, 8):
+        count = min(8, VIEWS - first)
+        tiles = assemble(NZ * NB // LANES, [(readers[z], first // 8 * NB, z * NB, NB) for z in range(NZ)], 8)
+        for t, tile in enumerate(tiles):
+            o_ref[0, first : first + count, t * LANES : (t + 1) * LANES] = tile[:count].astype(BF16)
 
 
 def pack(mine, yh, kernel_blocks, density):
@@ -268,6 +280,18 @@
     )(parts)
 
 
+def place(tiles):
+    vmem = pl.BlockSpec(memory_space=pltpu.VMEM)
+    return pl.pallas_call(
+        place_kernel,
+        in_specs=[vmem],
+        out_specs=vmem,
+        out_shape=jax.ShapeDtypeStruct((1, VIEWS, NZ * NB), BF16),
+        compiler_params=pltpu.CompilerParams(vmem_limit_bytes=VMEM_BYTES),
+        name="place",
+    )(tiles)
+
+
 def local(density, kernel_blocks):
     yh, yl, x, co = (lax.axis_index(name).astype(jnp.int32) for name in ("yh",) + ANGLE)
     mine = ((yl ^ yh) * 4 + x) * 2 + co
@@ -278,9 +302,7 @@
     own, other = project(yh.reshape(1), co.reshape(1), both, k2, d)
     parts = own + lax.ppermute(other, "co", [(0, 1), (1, 0)])
     parts = lax.all_to_all(parts, ("yl", "x"), 0, 0, tiled=True)
-    out = lax.all_to_all(fold(parts), Z, 0, 0, tiled=True)
-    out = out.reshape(NZ, -1)[:, : VIEWS * NB].reshape(NZ, VIEWS, NB)
-    return out.transpose(1, 0, 2).reshape(1, VIEWS, NZ * NB)
+    return place(lax.all_to_all(fold(parts), Z, 0, 0, tiled=True))
 
 
 def solution(mesh):

time: 102 us -> 102 us (level)
  no operation moved by 1% of the time
where the time goes in v7:
time: 102 us
  blocking collectives  74.1 us (73%)
  starting transfers between devices  10.3 us (10%)
  Pallas kernels  8.58 us (8%)
  waiting for transfers between devices  8.5 us (8%)
    all_to_all x1, blocking collectives, local(): lax.all_to_all(pack(mine.reshape(1), yh.reshape(1), kernel_blocks, densit...  38.8 us
    all_to_all x1, blocking collectives, local(): return place(lax.all_to_all(fold(parts), Z, 0, 0, tiled=True))  19.4 us
    all_to_all x1, blocking collectives, local(): parts = lax.all_to_all(parts, ('yl', 'x'), 0, 0, tiled=True)  16 us
    ppermute x1, waiting for transfers between devices, local(): k2 = lax.ppermute(k2, ('yh', 'yl'), [(0, 3), (1, 2), (2, 1), (3, 0)])  6.8 us
    all_to_all x1, starting transfers between devices, local(): d = lax.all_to_all(d, ('zb',) + ANGLE, 0, 0, tiled=True)  5.41 us
    pallas_call x1, Pallas kernels, project(): pl.pallas_call(main_kernel, in_specs=[smem, smem, vmem, vmem, vmem], out_...  5.25 us
    ppermute x1, starting transfers between devices, local(): k2 = lax.ppermute(k2, ('yh', 'yl'), [(0, 3), (1, 2), (2, 1), (3, 0)])  2.87 us
    ppermute x1, starting transfers between devices, local(): parts = own + lax.ppermute(other, 'co', [(0, 1), (1, 0)])  2.06 us
  transfers between devices with their start and end apart: 3, of which 3 were waited for; matrix products, arithmetic and copies ran while one was open for 0% of the time, Pallas kernels for 0%

profile of v7, /device:TPU:16, one launch (start us, length us, event | category | flops | bytes accessed | tf_op | source)
XLA Modules:
  0.0 101.7 jit_solution(3176086247582874946)
XLA Ops:
  0.0 1.3 %pack.1 = bf16[16,6,16,128]{3,2,1,0:T(8,128)(2,1)S(1)} custom-call(s32[1]{0:T(128)} %bitcast.2.mine_ref, s32[1]{0:T(128)} %bitcast.yh_ref, bf16[18,256,384]{2,1,0:T(8,128)(2,1)} %k_hbm.1, bf16[1,36,256]{2,1,0:T(8,128)(2,1)} %d_hbm.1), custom_call_target="tpu_custom_call" | custom-call | tf_op jit(solution)/shard_map/pack/pallas_call | solution.py:218
  1.4 38.8 %all_to_all.20.k_ref.k1_ref = bf16[16,6,16,128]{3,2,1,0:T(8,128)(2,1)S(1)} all-to-all(bf16[16,6,16,128]{3,2,1,0:T(8,128)(2,1)S(1)} %pack.1), channel_id=1, replica_groups=mesh['zp'=8,'zb'=2,'yh'=2,'yl'=2,'x'=4,'co'=2] {'zp','zb'}, dimensions={0} | all-to-all | bytes 786432 | tf_op jit(solution)/shard_map/all_to_all | solution.py:298
  40.1 0.1 copy.3.d_ref
  40.2 1.1 %regroup.1 = (bf16[32,3,16,128]{3,2,1,0:T(8,128)(2,1)}, bf16[56,16,128]{2,1,0:T(8,128)(2,1)S(1)}) custom-call(bf16[16,6,16,128]{3,2,1,0:T(8,128)(2,1)S(1)} %all_to_all.20.k_ref.k1_ref, bf16[3,16,16,128]{3,2,1,0:T(8,128)(2,1)S(1)} %copy.3.d_ref), custom_call_target="tpu_custom_call" | custom-call | tf_op jit(solution)/shard_map/regroup/pallas_call | solution.py:236
  41.3 5.4 %all-to-all-start.1 = ((bf16[32,3,16,128]{3,2,1,0:T(8,128)(2,1)}), bf16[32,3,16,128]{3,2,1,0:T(8,128)(2,1)S(1)}, u32[]{:S(2)}, u32[]{:S(2)}) async-start(bf16[32,3,16,128]{3,2,1,0:T(8,128)(2,1)} %get-tuple-element.10), calls=%async_computation.1 | async-start | bytes 786432 | tf_op jit(solution)/shard_map/all_to_all | solution.py:301
  46.7 2.9 %collective-permute-start = (bf16[56,16,128]{2,1,0:T(8,128)(2,1)S(1)}, bf16[56,16,128]{2,1,0:T(8,128)(2,1)S(1)}, u32[]{:S(2)}, u32[]{:S(2)}) collective-permute-start(bf16[56,16,128]{2,1,0:T(8,128)(2,1)S(1)} %get-tuple-element.9), channel_id=1, source_target_pairs={{0,24},{8,16},{16,8},{24,0},{1,25},{9,17},{17,9},{25,1},{2,26},{10... | collective-permute-start | bytes 688136 | tf_op jit(solution)/shard_map/ppermute | solution.py:300
  49.6 6.8 %collective-permute-done.k2_ref = bf16[56,16,128]{2,1,0:T(8,128)(2,1)S(1)} collective-permute-done((bf16[56,16,128]{2,1,0:T(8,128)(2,1)S(1)}, bf16[56,16,128]{2,1,0:T(8,128)(2,1)S(1)}, u32[]{:S(2)}, u32[]{:S(2)}) %collective-permute-start) | collective-permute-done | bytes 229408 | tf_op jit(solution)/shard_map/ppermute | solution.py:300
  56.4 0.1 all-to-all-done.1.d_ref
  56.4 5.2 %project.1 = (f32[8,16,864]{2,1,0:T(8,128)S(1)}, f32[8,16,864]{2,1,0:T(8,128)S(1)}) custom-call(s32[1]{0:T(128)} %bitcast.yh_ref, s32[1]{0:T(128)} %bitcast.1.co_ref, bf16[16,6,16,128]{3,2,1,0:T(8,128)(2,1)S(1)} %all_to_all.20.k_ref.k1_ref, bf16[56,16,128]{2,1,0:T(8,128)(2,1)S(1)} %collective-permute-done.k2_ref, ...), custom_call_target="tpu_custom_call" | custom-call | tf_op jit(solution)/shard_map/project/pallas_call | solution.py:254
  61.7 2.1 %collective-permute-start.1 = (f32[8,16,864]{2,1,0:T(8,128)S(1)}, f32[8,16,864]{2,1,0:T(8,128)S(1)}, u32[]{:S(2)}, u32[]{:S(2)}) collective-permute-start(f32[8,16,864]{2,1,0:T(8,128)S(1)} %get-tuple-element.12), channel_id=1, source_target_pairs={{0,1},{1,0},{2,3},{3,2},{4,5},{5,4},{6,7},{7,6},{8,9},{9,8},{10,11... | collective-permute-start | bytes 1327112 | tf_op jit(solution)/shard_map/ppermute | solution.py:303
  63.8 1.6 %collective-permute-done.1 = f32[8,16,864]{2,1,0:T(8,128)S(1)} collective-permute-done((f32[8,16,864]{2,1,0:T(8,128)S(1)}, f32[8,16,864]{2,1,0:T(8,128)S(1)}, u32[]{:S(2)}, u32[]{:S(2)}) %collective-permute-start.1) | collective-permute-done | bytes 442400 | tf_op jit(solution)/shard_map/ppermute | solution.py:303
  65.4 0.1 add.11
  65.5 16.0 %all_to_all.21.p_ref = f32[8,16,864]{2,1,0:T(8,128)S(1)} all-to-all(f32[8,16,864]{2,1,0:T(8,128)S(1)} %add.11), channel_id=1, replica_groups=mesh['zp'=8,'zb'=2,'yh'=2,'yl'=2,'x'=4,'co'=2] {'yl','x'}, dimensions={0} | all-to-all | bytes 884736 | tf_op jit(solution)/shard_map/all_to_all | solution.py:304
  81.5 0.2 fold.1
  81.6 19.4 %all_to_all.22.t_ref = bf16[16,8,128]{2,1,0:T(8,128)(2,1)S(1)} all-to-all(bf16[16,8,128]{2,1,0:T(8,128)(2,1)S(1)} %fold.1), channel_id=1, replica_groups=mesh['zp'=8,'zb'=2,'yh'=2,'yl'=2,'x'=4,'co'=2] {'zp','zb'}, dimensions={0} | all-to-all | bytes 65536 | tf_op jit(solution)/shard_map/all_to_all | solution.py:305
  101.0 0.7 place.1
  (1 shorter events, 0.0 us)
Async XLA Ops:
  41.3 15.1 %all-to-all-start.1 = ((bf16[32,3,16,128]{3,2,1,0:T(8,128)(2,1)}), bf16[32,3,16,128]{3,2,1,0:T(8,128)(2,1)S(1)}, u32[]{:S(2)}, u32[]{:S(2)}) async-start(bf16[32,3,16,128]{3,2,1,0:T(8,128)(2,1)} %get-tuple-element.10), calls=%async_computation.1 | async-start | bytes 786432 | tf_op jit(solution)/shard_map/all_to_all | solution.py:301
  46.7 9.7 %collective-permute-start = (bf16[56,16,128]{2,1,0:T(8,128)(2,1)S(1)}, bf16[56,16,128]{2,1,0:T(8,128)(2,1)S(1)}, u32[]{:S(2)}, u32[]{:S(2)}) collective-permute-start(bf16[56,16,128]{2,1,0:T(8,128)(2,1)S(1)} %get-tuple-element.9), channel_id=1, source_target_pairs={{0,24},{8,16},{16,8},{24,0},{1,25},{9,17},{17,9},{25,1},{2,26},{10... | collective-permute-start | bytes 688136 | tf_op jit(solution)/shard_map/ppermute | solution.py:300
  61.7 3.7 %collective-permute-start.1 = (f32[8,16,864]{2,1,0:T(8,128)S(1)}, f32[8,16,864]{2,1,0:T(8,128)S(1)}, u32[]{:S(2)}, u32[]{:S(2)}) collective-permute-start(f32[8,16,864]{2,1,0:T(8,128)S(1)} %get-tuple-element.12), channel_id=1, source_target_pairs={{0,1},{1,0},{2,3},{3,2},{4,5},{5,4},{6,7},{7,6},{8,9},{9,8},{10,11... | collective-permute-start | bytes 1327112 | tf_op jit(solution)/shard_map/ppermute | solution.py:303

commit v8 on v7

--- a/solution.py
+++ b/solution.py
@@ -108,33 +108,8 @@
         swap_ref[NZ * 3 + z // 2] = jnp.where(lane < TAIL, k_ref[z, 3], rotate(k_ref[z + 1, 3], TAIL))
 
 
-def main_kernel(yh_ref, co_ref, k1_ref, k2_ref, d_ref, own_ref, other_ref, flat, weights, paired, left):
-    half = OFFSETS * NB
-    group = NR * NB // LANES
-    tiles_all = 2 * NZ * half // LANES
-    blocks = tiles_all // group
-    width = own_ref.shape[2]
-    lane = lax.broadcasted_iota(jnp.int32, (ROWS, LANES), 1)
-    first = yh_ref[0] == 0
-
-    def reader(z, h):
-        def load(t):
-            a = k1_ref[z, t].astype(F32)
-            b = k2_ref[z * 3 + t if t < 3 else NZ * 3 + z // 2].astype(F32)
-            if t == 3 and z % 2:
-                b = rotate(b, -TAIL)
-            return jnp.where(first, a, b) if h == 0 else jnp.where(first, b, a)
-
-        return cached(load)
-
-    tiles = assemble(
-        tiles_all, [(reader(z, h), 0, (2 * z + h) * half, half) for z in range(NZ) for h in range(2)]
-    )
-    for t in range(tiles_all):
-        flat[t + group] = tiles[t]
-    for t in range(group):
-        flat[t] = tiles[tiles_all - group + t]
-
+def rows_kernel(d_ref, left):
+    blocks = left.shape[0] // (2 * NZ)
     span = PART * NR
     tiles = assemble(
         blocks * 2,
@@ -150,6 +125,34 @@
             for rep in range(2):
                 row = (rep * blocks + w) * NZ
                 left[row : row + NZ, t * LANES : (t + 1) * LANES] = tile
+
+
+def main_kernel(yh_ref, co_ref, k1_ref, k2_ref, left, own_ref, other_ref, flat, weights, paired):
+    half = OFFSETS * NB
+    group = NR * NB // LANES
+    tiles_all = 2 * NZ * half // LANES
+    blocks = tiles_all // group
+    width = own_ref.shape[2]
+    lane = lax.broadcasted_iota(jnp.int32, (ROWS, LANES), 1)
+    first = yh_ref[0] == 0
+
+    def reader(z, h):
+        def load(t):
+            a = k1_ref[z, t].astype(F32)
+            b = k2_ref[z * 3 + t if t < 3 else NZ * 3 + z // 2].astype(F32)
+            if t == 3 and z % 2:
+                b = rotate(b, -TAIL)
+            return jnp.where(first, a, b) if h == 0 else jnp.where(first, b, a)
+
+        return cached(load)
+
+    tiles = assemble(
+        tiles_all, [(reader(z, h), 0, (2 * z + h) * half, half) for z in range(NZ) for h in range(2)]
+    )
+    for t in range(tiles_all):
+        flat[t + group] = tiles[t]
+    for t in range(group):
+        flat[t] = tiles[tiles_all - group + t]
 
     for block in range(blocks):
         for j in range(NR):
@@ -246,6 +249,18 @@
     )(both, d)
 
 
+def density_rows(d):
+    vmem = pl.BlockSpec(memory_space=pltpu.VMEM)
+    return pl.pallas_call(
+        rows_kernel,
+        in_specs=[vmem],
+        out_specs=vmem,
+        out_shape=jax.ShapeDtypeStruct((2 * NA * VIEWS * NZ // NR, NR * NR), BF16),
+        compiler_params=pltpu.CompilerParams(vmem_limit_bytes=VMEM_BYTES),
+        name="density_rows",
+    )(d)
+
+
 def project(yh, co, k1, k2, d):
     half = OFFSETS * NB
     blocks = 2 * NZ * half // (NR * NB)
@@ -260,7 +275,6 @@
             pltpu.VMEM((2 * NZ * half // LANES + NR * NB // LANES, ROWS, LANES), F32),
             pltpu.VMEM((blocks * NR * NR, 2 * LANES), BF16),
             pltpu.VMEM((blocks // 2 * NR * NR, 2 * LANES), BF16),
-            pltpu.VMEM((2 * blocks * NZ, NR * NR), BF16),
         ],
         compiler_params=pltpu.CompilerParams(vmem_limit_bytes=VMEM_BYTES),
         name="project",
@@ -299,7 +313,7 @@
     d, k2 = regroup(both)
     k2 = lax.ppermute(k2, ("yh", "yl"), [(0, 3), (1, 2), (2, 1), (3, 0)])
     d = lax.all_to_all(d, ("zb",) + ANGLE, 0, 0, tiled=True)
-    own, other = project(yh.reshape(1), co.reshape(1), both, k2, d)
+    own, other = project(yh.reshape(1), co.reshape(1), both, k2, density_rows(d))
     parts = own + lax.ppermute(other, "co", [(0, 1), (1, 0)])
     parts = lax.all_to_all(parts, ("yl", "x"), 0, 0, tiled=True)
     return place(lax.all_to_all(fold(parts), Z, 0, 0, tiled=True))

time: 102 us -> 102 us (level)
    all_to_all x1, waiting for transfers between devices: 0.05 us -> 6.85 us  [local(): d = lax.all_to_all(d, ('zb',) + ANGLE, 0, 0, tiled=True)]
    ppermute x1, waiting for transfers between devices: 6.8 us -> 0.01 us  [local(): k2 = lax.ppermute(k2, ('yh', 'yl'), [(0, 3), (1, 2), (2, 1), (3, 0)])]
  transfers between devices with their start and end apart: 3 -> 3, of which waited for: 3 -> 2; matrix products, arithmetic and copies ran while one was open for 0% -> 0% of each run, Pallas kernels for 0% -> 0%
where the time goes in v8:
time: 102 us
  blocking collectives  74 us (73%)
  starting transfers between devices  10.3 us (10%)
  Pallas kernels  8.73 us (9%)
  waiting for transfers between devices  8.5 us (8%)
    all_to_all x1, blocking collectives, local(): lax.all_to_all(pack(mine.reshape(1), yh.reshape(1), kernel_blocks, densit...  38.8 us
    all_to_all x1, blocking collectives, local(): return place(lax.all_to_all(fold(parts), Z, 0, 0, tiled=True))  19.4 us
    all_to_all x1, blocking collectives, local(): parts = lax.all_to_all(parts, ('yl', 'x'), 0, 0, tiled=True)  15.8 us
    all_to_all x1, waiting for transfers between devices, local(): d = lax.all_to_all(d, ('zb',) + ANGLE, 0, 0, tiled=True)  6.85 us
    all_to_all x1, starting transfers between devices, local(): d = lax.all_to_all(d, ('zb',) + ANGLE, 0, 0, tiled=True)  5.41 us
    pallas_call x1, Pallas kernels, project(): pl.pallas_call(main_kernel, in_specs=[smem, smem, vmem, vmem, vmem], out_...  5.24 us
    ppermute x1, starting transfers between devices, local(): k2 = lax.ppermute(k2, ('yh', 'yl'), [(0, 3), (1, 2), (2, 1), (3, 0)])  2.87 us
    ppermute x1, starting transfers between devices, local(): parts = own + lax.ppermute(other, 'co', [(0, 1), (1, 0)])  2.06 us
  transfers between devices with their start and end apart: 3, of which 2 were waited for; matrix products, arithmetic and copies ran while one was open for 0% of the time, Pallas kernels for 0%

profile of v8, /device:TPU:16, one launch (start us, length us, event | category | flops | bytes accessed | tf_op | source)
XLA Modules:
  0.0 101.7 jit_solution(12914338373575749974)
XLA Ops:
  0.0 1.3 %pack.1 = bf16[16,6,16,128]{3,2,1,0:T(8,128)(2,1)S(1)} custom-call(s32[1]{0:T(128)} %bitcast.2.mine_ref, s32[1]{0:T(128)} %bitcast.yh_ref, bf16[18,256,384]{2,1,0:T(8,128)(2,1)} %k_hbm.1, bf16[1,36,256]{2,1,0:T(8,128)(2,1)} %d_hbm.1), custom_call_target="tpu_custom_call" | custom-call | tf_op jit(solution)/shard_map/pack/pallas_call | solution.py:221
  1.4 38.8 %all_to_all.20.k_ref.k1_ref = bf16[16,6,16,128]{3,2,1,0:T(8,128)(2,1)S(1)} all-to-all(bf16[16,6,16,128]{3,2,1,0:T(8,128)(2,1)S(1)} %pack.1), channel_id=1, replica_groups=mesh['zp'=8,'zb'=2,'yh'=2,'yl'=2,'x'=4,'co'=2] {'zp','zb'}, dimensions={0} | all-to-all | bytes 786432 | tf_op jit(solution)/shard_map/all_to_all | solution.py:312
  40.1 0.1 copy.3.d_ref
  40.2 1.1 %regroup.1 = (bf16[32,3,16,128]{3,2,1,0:T(8,128)(2,1)}, bf16[56,16,128]{2,1,0:T(8,128)(2,1)S(1)}) custom-call(bf16[16,6,16,128]{3,2,1,0:T(8,128)(2,1)S(1)} %all_to_all.20.k_ref.k1_ref, bf16[3,16,16,128]{3,2,1,0:T(8,128)(2,1)S(1)} %copy.3.d_ref), custom_call_target="tpu_custom_call" | custom-call | tf_op jit(solution)/shard_map/regroup/pallas_call | solution.py:239
  41.3 5.4 %all-to-all-start.1 = ((bf16[32,3,16,128]{3,2,1,0:T(8,128)(2,1)}), bf16[32,3,16,128]{3,2,1,0:T(8,128)(2,1)S(1)}, u32[]{:S(2)}, u32[]{:S(2)}) async-start(bf16[32,3,16,128]{3,2,1,0:T(8,128)(2,1)} %get-tuple-element.10), calls=%async_computation.1 | async-start | bytes 786432 | tf_op jit(solution)/shard_map/all_to_all | solution.py:315
  46.7 2.9 %collective-permute-start = (bf16[56,16,128]{2,1,0:T(8,128)(2,1)S(1)}, bf16[56,16,128]{2,1,0:T(8,128)(2,1)S(1)}, u32[]{:S(2)}, u32[]{:S(2)}) collective-permute-start(bf16[56,16,128]{2,1,0:T(8,128)(2,1)S(1)} %get-tuple-element.9), channel_id=1, source_target_pairs={{0,24},{8,16},{16,8},{24,0},{1,25},{9,17},{17,9},{25,1},{2,26},{10... | collective-permute-start | bytes 688136 | tf_op jit(solution)/shard_map/ppermute | solution.py:314
  49.6 6.9 %all-to-all-done.1.d_ref = bf16[32,3,16,128]{3,2,1,0:T(8,128)(2,1)S(1)} async-done(((bf16[32,3,16,128]{3,2,1,0:T(8,128)(2,1)}), bf16[32,3,16,128]{3,2,1,0:T(8,128)(2,1)S(1)}, u32[]{:S(2)}, u32[]{:S(2)}) %all-to-all-start.1) | async-done | bytes 393248 | tf_op jit(solution)/shard_map/all_to_all | solution.py:315
  56.4 0.2 density_rows.1.left
  56.6 0.0 collective-permute-done.k2_ref
  56.6 5.2 %project.1 = (f32[8,16,864]{2,1,0:T(8,128)S(1)}, f32[8,16,864]{2,1,0:T(8,128)S(1)}) custom-call(s32[1]{0:T(128)} %bitcast.yh_ref, s32[1]{0:T(128)} %bitcast.1.co_ref, bf16[16,6,16,128]{3,2,1,0:T(8,128)(2,1)S(1)} %all_to_all.20.k_ref.k1_ref, bf16[56,16,128]{2,1,0:T(8,128)(2,1)S(1)} %collective-permute-done.k2_ref, bf16[1152,256]{1,0:T(8,128)(2,1)S(1)} %density_rows.1.left), custom_call_target="tpu_custom_call" | custom-call | tf_op jit(solution)/shard_map/project/pallas_call | solution.py:269
  61.8 2.1 %collective-permute-start.1 = (f32[8,16,864]{2,1,0:T(8,128)S(1)}, f32[8,16,864]{2,1,0:T(8,128)S(1)}, u32[]{:S(2)}, u32[]{:S(2)}) collective-permute-start(f32[8,16,864]{2,1,0:T(8,128)S(1)} %get-tuple-element.12), channel_id=1, source_target_pairs={{0,1},{1,0},{2,3},{3,2},{4,5},{5,4},{6,7},{7,6},{8,9},{9,8},{10,11... | collective-permute-start | bytes 1327112 | tf_op jit(solution)/shard_map/ppermute | solution.py:317
  63.9 1.6 %collective-permute-done.1 = f32[8,16,864]{2,1,0:T(8,128)S(1)} collective-permute-done((f32[8,16,864]{2,1,0:T(8,128)S(1)}, f32[8,16,864]{2,1,0:T(8,128)S(1)}, u32[]{:S(2)}, u32[]{:S(2)}) %collective-permute-start.1) | collective-permute-done | bytes 442400 | tf_op jit(solution)/shard_map/ppermute | solution.py:317
  65.6 0.1 add.11
  65.6 15.8 %all_to_all.21.p_ref = f32[8,16,864]{2,1,0:T(8,128)S(1)} all-to-all(f32[8,16,864]{2,1,0:T(8,128)S(1)} %add.11), channel_id=1, replica_groups=mesh['zp'=8,'zb'=2,'yh'=2,'yl'=2,'x'=4,'co'=2] {'yl','x'}, dimensions={0} | all-to-all | bytes 884736 | tf_op jit(solution)/shard_map/all_to_all | solution.py:318
  81.4 0.2 fold.1
  81.6 19.4 %all_to_all.22.t_ref = bf16[16,8,128]{2,1,0:T(8,128)(2,1)S(1)} all-to-all(bf16[16,8,128]{2,1,0:T(8,128)(2,1)S(1)} %fold.1), channel_id=1, replica_groups=mesh['zp'=8,'zb'=2,'yh'=2,'yl'=2,'x'=4,'co'=2] {'zp','zb'}, dimensions={0} | all-to-all | bytes 65536 | tf_op jit(solution)/shard_map/all_to_all | solution.py:319
  101.0 0.7 place.1
  (1 shorter events, 0.0 us)
Async XLA Ops:
  41.3 15.1 %all-to-all-start.1 = ((bf16[32,3,16,128]{3,2,1,0:T(8,128)(2,1)}), bf16[32,3,16,128]{3,2,1,0:T(8,128)(2,1)S(1)}, u32[]{:S(2)}, u32[]{:S(2)}) async-start(bf16[32,3,16,128]{3,2,1,0:T(8,128)(2,1)} %get-tuple-element.10), calls=%async_computation.1 | async-start | bytes 786432 | tf_op jit(solution)/shard_map/all_to_all | solution.py:315
  46.7 9.9 %collective-permute-start = (bf16[56,16,128]{2,1,0:T(8,128)(2,1)S(1)}, bf16[56,16,128]{2,1,0:T(8,128)(2,1)S(1)}, u32[]{:S(2)}, u32[]{:S(2)}) collective-permute-start(bf16[56,16,128]{2,1,0:T(8,128)(2,1)S(1)} %get-tuple-element.9), channel_id=1, source_target_pairs={{0,24},{8,16},{16,8},{24,0},{1,25},{9,17},{17,9},{25,1},{2,26},{10... | collective-permute-start | bytes 688136 | tf_op jit(solution)/shard_map/ppermute | solution.py:314
  61.8 3.7 %collective-permute-start.1 = (f32[8,16,864]{2,1,0:T(8,128)S(1)}, f32[8,16,864]{2,1,0:T(8,128)S(1)}, u32[]{:S(2)}, u32[]{:S(2)}) collective-permute-start(f32[8,16,864]{2,1,0:T(8,128)S(1)} %get-tuple-element.12), channel_id=1, source_target_pairs={{0,1},{1,0},{2,3},{3,2},{4,5},{5,4},{6,7},{7,6},{8,9},{9,8},{10,11... | collective-permute-start | bytes 1327112 | tf_op jit(solution)/shard_map/ppermute | solution.py:317

commit v9 on v7

--- a/solution.py
+++ b/solution.py
@@ -185,8 +185,8 @@
         for t in range(count):
             w = min(LANES, width - t * LANES)
             even, odd = (p[t][:, :w] for p in pair)
-            own_ref[n, :, t * LANES : t * LANES + w] = jnp.where(one, odd, even)
-            other_ref[n, :, t * LANES : t * LANES + w] = jnp.where(one, even, odd)
+            own_ref[n % 4 * 2 + n // 4, :, t * LANES : t * LANES + w] = jnp.where(one, odd, even)
+            other_ref[n % 4 * 2 + n // 4, :, t * LANES : t * LANES + w] = jnp.where(one, even, odd)
 
 
 def fold_kernel(p_ref, o_ref, rows):
@@ -301,7 +301,7 @@
     d = lax.all_to_all(d, ("zb",) + ANGLE, 0, 0, tiled=True)
     own, other = project(yh.reshape(1), co.reshape(1), both, k2, d)
     parts = own + lax.ppermute(other, "co", [(0, 1), (1, 0)])
-    parts = lax.all_to_all(parts, ("yl", "x"), 0, 0, tiled=True)
+    parts = lax.all_to_all(parts, ("x", "yl"), 0, 0, tiled=True)
     return place(lax.all_to_all(fold(parts), Z, 0, 0, tiled=True))
 
 

time: 102 us -> 102 us (level)
  no operation moved by 1% of the time
where the time goes in v9:
time: 102 us; the launch traced here: 101 us
  blocking collectives  73.9 us (72%)
  starting transfers between devices  10.3 us (10%)
  Pallas kernels  8.58 us (8%)
  waiting for transfers between devices  8.5 us (8%)
    all_to_all x1, blocking collectives, local(): lax.all_to_all(pack(mine.reshape(1), yh.reshape(1), kernel_blocks, densit...  38.8 us
    all_to_all x1, blocking collectives, local(): return place(lax.all_to_all(fold(parts), Z, 0, 0, tiled=True))  19.4 us
    all_to_all x1, blocking collectives, local(): parts = lax.all_to_all(parts, ('x', 'yl'), 0, 0, tiled=True)  15.7 us
    ppermute x1, waiting for transfers between devices, local(): k2 = lax.ppermute(k2, ('yh', 'yl'), [(0, 3), (1, 2), (2, 1), (3, 0)])  6.8 us
    all_to_all x1, starting transfers between devices, local(): d = lax.all_to_all(d, ('zb',) + ANGLE, 0, 0, tiled=True)  5.41 us
    pallas_call x1, Pallas kernels, project(): pl.pallas_call(main_kernel, in_specs=[smem, smem, vmem, vmem, vmem], out_...  5.25 us
    ppermute x1, starting transfers between devices, local(): k2 = lax.ppermute(k2, ('yh', 'yl'), [(0, 3), (1, 2), (2, 1), (3, 0)])  2.87 us
    ppermute x1, starting transfers between devices, local(): parts = own + lax.ppermute(other, 'co', [(0, 1), (1, 0)])  2.06 us
  transfers between devices with their start and end apart: 3, of which 3 were waited for; matrix products, arithmetic and copies ran while one was open for 0% of the time, Pallas kernels for 0%

profile of v9, /device:TPU:16, one launch (start us, length us, event | category | flops | bytes accessed | tf_op | source)
XLA Modules:
  0.0 101.5 jit_solution(424331394677774901)
XLA Ops:
  0.0 1.3 %pack.1 = bf16[16,6,16,128]{3,2,1,0:T(8,128)(2,1)S(1)} custom-call(s32[1]{0:T(128)} %bitcast.2.mine_ref, s32[1]{0:T(128)} %bitcast.yh_ref, bf16[18,256,384]{2,1,0:T(8,128)(2,1)} %k_hbm.1, bf16[1,36,256]{2,1,0:T(8,128)(2,1)} %d_hbm.1), custom_call_target="tpu_custom_call" | custom-call | tf_op jit(solution)/shard_map/pack/pallas_call | solution.py:218
  1.4 38.8 %all_to_all.20.k_ref.k1_ref = bf16[16,6,16,128]{3,2,1,0:T(8,128)(2,1)S(1)} all-to-all(bf16[16,6,16,128]{3,2,1,0:T(8,128)(2,1)S(1)} %pack.1), channel_id=1, replica_groups=mesh['zp'=8,'zb'=2,'yh'=2,'yl'=2,'x'=4,'co'=2] {'zp','zb'}, dimensions={0} | all-to-all | bytes 786432 | tf_op jit(solution)/shard_map/all_to_all | solution.py:298
  40.1 0.1 copy.3.d_ref
  40.2 1.1 %regroup.1 = (bf16[32,3,16,128]{3,2,1,0:T(8,128)(2,1)}, bf16[56,16,128]{2,1,0:T(8,128)(2,1)S(1)}) custom-call(bf16[16,6,16,128]{3,2,1,0:T(8,128)(2,1)S(1)} %all_to_all.20.k_ref.k1_ref, bf16[3,16,16,128]{3,2,1,0:T(8,128)(2,1)S(1)} %copy.3.d_ref), custom_call_target="tpu_custom_call" | custom-call | tf_op jit(solution)/shard_map/regroup/pallas_call | solution.py:236
  41.3 5.4 %all-to-all-start.1 = ((bf16[32,3,16,128]{3,2,1,0:T(8,128)(2,1)}), bf16[32,3,16,128]{3,2,1,0:T(8,128)(2,1)S(1)}, u32[]{:S(2)}, u32[]{:S(2)}) async-start(bf16[32,3,16,128]{3,2,1,0:T(8,128)(2,1)} %get-tuple-element.10), calls=%async_computation.1 | async-start | bytes 786432 | tf_op jit(solution)/shard_map/all_to_all | solution.py:301
  46.7 2.9 %collective-permute-start = (bf16[56,16,128]{2,1,0:T(8,128)(2,1)S(1)}, bf16[56,16,128]{2,1,0:T(8,128)(2,1)S(1)}, u32[]{:S(2)}, u32[]{:S(2)}) collective-permute-start(bf16[56,16,128]{2,1,0:T(8,128)(2,1)S(1)} %get-tuple-element.9), channel_id=1, source_target_pairs={{0,24},{8,16},{16,8},{24,0},{1,25},{9,17},{17,9},{25,1},{2,26},{10... | collective-permute-start | bytes 688136 | tf_op jit(solution)/shard_map/ppermute | solution.py:300
  49.6 6.8 %collective-permute-done.k2_ref = bf16[56,16,128]{2,1,0:T(8,128)(2,1)S(1)} collective-permute-done((bf16[56,16,128]{2,1,0:T(8,128)(2,1)S(1)}, bf16[56,16,128]{2,1,0:T(8,128)(2,1)S(1)}, u32[]{:S(2)}, u32[]{:S(2)}) %collective-permute-start) | collective-permute-done | bytes 229408 | tf_op jit(solution)/shard_map/ppermute | solution.py:300
  56.4 0.1 all-to-all-done.1.d_ref
  56.4 5.2 %project.1 = (f32[8,16,864]{2,1,0:T(8,128)S(1)}, f32[8,16,864]{2,1,0:T(8,128)S(1)}) custom-call(s32[1]{0:T(128)} %bitcast.yh_ref, s32[1]{0:T(128)} %bitcast.1.co_ref, bf16[16,6,16,128]{3,2,1,0:T(8,128)(2,1)S(1)} %all_to_all.20.k_ref.k1_ref, bf16[56,16,128]{2,1,0:T(8,128)(2,1)S(1)} %collective-permute-done.k2_ref, ...), custom_call_target="tpu_custom_call" | custom-call | tf_op jit(solution)/shard_map/project/pallas_call | solution.py:254
  61.7 2.1 %collective-permute-start.1 = (f32[8,16,864]{2,1,0:T(8,128)S(1)}, f32[8,16,864]{2,1,0:T(8,128)S(1)}, u32[]{:S(2)}, u32[]{:S(2)}) collective-permute-start(f32[8,16,864]{2,1,0:T(8,128)S(1)} %get-tuple-element.12), channel_id=1, source_target_pairs={{0,1},{1,0},{2,3},{3,2},{4,5},{5,4},{6,7},{7,6},{8,9},{9,8},{10,11... | collective-permute-start | bytes 1327112 | tf_op jit(solution)/shard_map/ppermute | solution.py:303
  63.8 1.6 %collective-permute-done.1 = f32[8,16,864]{2,1,0:T(8,128)S(1)} collective-permute-done((f32[8,16,864]{2,1,0:T(8,128)S(1)}, f32[8,16,864]{2,1,0:T(8,128)S(1)}, u32[]{:S(2)}, u32[]{:S(2)}) %collective-permute-start.1) | collective-permute-done | bytes 442400 | tf_op jit(solution)/shard_map/ppermute | solution.py:303
  65.4 0.1 add.11
  65.5 15.7 %all_to_all.21.p_ref = f32[8,16,864]{2,1,0:T(8,128)S(1)} all-to-all(f32[8,16,864]{2,1,0:T(8,128)S(1)} %add.11), channel_id=1, replica_groups=mesh['zp'=8,'zb'=2,'yh'=2,'yl'=2,'x'=4,'co'=2] {'x','yl'}, dimensions={0} | all-to-all | bytes 884736 | tf_op jit(solution)/shard_map/all_to_all | solution.py:304
  81.2 0.2 fold.1
  81.4 19.4 %all_to_all.22.t_ref = bf16[16,8,128]{2,1,0:T(8,128)(2,1)S(1)} all-to-all(bf16[16,8,128]{2,1,0:T(8,128)(2,1)S(1)} %fold.1), channel_id=1, replica_groups=mesh['zp'=8,'zb'=2,'yh'=2,'yl'=2,'x'=4,'co'=2] {'zp','zb'}, dimensions={0} | all-to-all | bytes 65536 | tf_op jit(solution)/shard_map/all_to_all | solution.py:305
  100.8 0.7 place.1
  (1 shorter events, 0.0 us)
Async XLA Ops:
  41.3 15.1 %all-to-all-start.1 = ((bf16[32,3,16,128]{3,2,1,0:T(8,128)(2,1)}), bf16[32,3,16,128]{3,2,1,0:T(8,128)(2,1)S(1)}, u32[]{:S(2)}, u32[]{:S(2)}) async-start(bf16[32,3,16,128]{3,2,1,0:T(8,128)(2,1)} %get-tuple-element.10), calls=%async_computation.1 | async-start | bytes 786432 | tf_op jit(solution)/shard_map/all_to_all | solution.py:301
  46.7 9.7 %collective-permute-start = (bf16[56,16,128]{2,1,0:T(8,128)(2,1)S(1)}, bf16[56,16,128]{2,1,0:T(8,128)(2,1)S(1)}, u32[]{:S(2)}, u32[]{:S(2)}) collective-permute-start(bf16[56,16,128]{2,1,0:T(8,128)(2,1)S(1)} %get-tuple-element.9), channel_id=1, source_target_pairs={{0,24},{8,16},{16,8},{24,0},{1,25},{9,17},{17,9},{25,1},{2,26},{10... | collective-permute-start | bytes 688136 | tf_op jit(solution)/shard_map/ppermute | solution.py:300
  61.7 3.7 %collective-permute-start.1 = (f32[8,16,864]{2,1,0:T(8,128)S(1)}, f32[8,16,864]{2,1,0:T(8,128)S(1)}, u32[]{:S(2)}, u32[]{:S(2)}) collective-permute-start(f32[8,16,864]{2,1,0:T(8,128)S(1)} %get-tuple-element.12), channel_id=1, source_target_pairs={{0,1},{1,0},{2,3},{3,2},{4,5},{5,4},{6,7},{7,6},{8,9},{9,8},{10,11... | collective-permute-start | bytes 1327112 | tf_op jit(solution)/shard_map/ppermute | solution.py:303
